TPU v7x, 128 devices: a whole 4x4x4 slice. The times are simulated.
128 devices in a mesh: frames: 2 (over y_hi), codebook: 16 (over y_lo, x, core), hidden: 4 (over z).
Axes of the slice: x: 4, y: 4 (y_hi: 2, y_lo: 2; y = y_hi * 2 + y_lo), z: 4, core: 2. Of those that a mesh axis runs over, the one named last changes fastest.
Arguments:
- temporal: bfloat16 [4096, 4096], P(('frames', 'codebook'), 'hidden'), may hold values from -6 to 6
- frame_ids: int32 [4096, 16], P('frames', 'codebook'), may hold values from 0 to 2047
- proj_weight: bfloat16 [16, 4096, 1024], P('codebook', 'hidden'), may hold values from -0.09375 to 0.09375
- embed_table: bfloat16 [16, 2049, 1024], P('codebook'), may hold values from -6 to 6
- qkv_weight: bfloat16 [16, 3, 1024, 1024], P('codebook', None, None, 'hidden'), may hold values from -12 to 12
- out_weight: bfloat16 [16, 1024, 1024], P('codebook', 'hidden'), may hold values from -0.1875 to 0.1875
- gate_up: bfloat16 [16, 2, 1024, 4096], P('codebook', None, None, 'hidden'), may hold values from -0.1875 to 0.1875
- down_weight: bfloat16 [16, 4096, 1024], P('codebook', 'hidden'), may hold values from -0.09375 to 0.09375
- norm_gains: float32 [16, 2, 1024], P('codebook'), may hold values from 0.25 to 1.75
Outputs:
- depth_states: float32 [16, 4096, 1024], P('codebook', 'frames', 'hidden')
All inputs are finite; a program needn't handle non-finite values.
Results may differ from a plain program's by a relative error of at most 0.015.
Values may be sent and summed in bfloat16 or wider, within the bound.
A program may use at most 192 MiB of HBM per device.

v0:
```python
import jax
import jax.numpy as jnp
from jax import lax
from jax.sharding import PartitionSpec as P

HEADS = 16


def shifted(block, axis, distance):
    devices = range(lax.axis_size(axis))
    route = [(i - distance, i) for i in devices if i - distance in devices]
    return lax.ppermute(block, axis, route)


def normalize(values, norm_gain):
    return values * lax.rsqrt(jnp.mean(values * values, axis=-1, keepdims=True) + 1e-05) * norm_gain


def gated(normed, piece):
    gate_sum = jnp.dot(normed, piece[0], preferred_element_type=jnp.float32)
    upper_sum = jnp.dot(normed, piece[1], preferred_element_type=jnp.float32)
    return (jax.nn.silu(gate_sum) * upper_sum).astype(jnp.bfloat16)


def body(
    temporal,
    frame_ids,
    proj_weight,
    embed_table,
    qkv_weight,
    out_weight,
    gate_up,
    down_weight,
    norm_gains,
):
    code_index = lax.axis_index("codebook")
    hidden_index = lax.axis_index("hidden")
    hidden_count = lax.axis_size("hidden")
    start_id = embed_table.shape[1] - 1
    token_table = embed_table[0]
    norm_gain = norm_gains[0]
    earlier = shifted(frame_ids, "codebook", 1)[:, 0]
    previous = jnp.where(code_index == 0, start_id, earlier)
    partial_sum = jnp.dot(
        lax.all_gather(temporal, "codebook", axis=0, tiled=True),
        proj_weight[0],
        preferred_element_type=jnp.float32,
    )
    row_count = partial_sum.shape[0]
    x_zero = lax.psum(partial_sum.astype(jnp.bfloat16), "hidden").astype(jnp.float32) + token_table[
        previous
    ].astype(jnp.float32)
    normed = normalize(x_zero, norm_gain[0]).astype(jnp.bfloat16)
    local_width = qkv_weight.shape[3]
    local_heads = HEADS // hidden_count
    head_size = local_width // local_heads
    triple = jnp.einsum(
        "rd,kdc->krc", normed, qkv_weight[0], preferred_element_type=jnp.float32
    ).astype(jnp.bfloat16)
    query_heads = triple[0].reshape(row_count, local_heads, head_size)
    highest = jnp.full((row_count, local_heads), -1e30, jnp.float32)
    key_piece = lax.all_gather(triple[1][None], "codebook", axis=0, tiled=True)
    value_piece = lax.all_gather(triple[2][None], "codebook", axis=0, tiled=True)
    positions = key_piece.shape[0]
    key_heads = key_piece.reshape(positions, row_count, local_heads, head_size)
    value_heads = value_piece.reshape(positions, row_count, local_heads, head_size)
    scores = jnp.einsum(
        "fhd,jfhd->jfh", query_heads, key_heads, preferred_element_type=jnp.float32
    ) * head_size ** (-0.5)
    valid = (jnp.arange(positions, dtype=jnp.int32) <= code_index)[:, None, None]
    scores = jnp.where(valid, scores, -1e30)
    new_highest = jnp.maximum(highest, jnp.max(scores, axis=0))
    weights = jnp.where(valid, jnp.exp(scores - new_highest[None]), 0.0)
    running = jnp.sum(weights, axis=0)
    summed = jnp.einsum(
        "jfh,jfhd->fhd",
        weights.astype(jnp.bfloat16),
        value_heads,
        preferred_element_type=jnp.float32,
    )
    highest, running, summed = (new_highest, running, summed)
    attended = (summed / running[..., None]).reshape(row_count, local_width).astype(jnp.bfloat16)
    attention_part = jnp.dot(attended, out_weight[0], preferred_element_type=jnp.float32)
    residual = x_zero + lax.psum(attention_part.astype(jnp.bfloat16), "hidden").astype(jnp.float32)
    normed_two = normalize(residual, norm_gain[1]).astype(jnp.bfloat16)
    activated = gated(normed_two, gate_up[0])
    down_part = jnp.dot(activated, down_weight[0], preferred_element_type=jnp.float32)
    mlp_piece = lax.psum_scatter(
        down_part.astype(jnp.bfloat16), "hidden", scatter_dimension=1, tiled=True
    ).astype(jnp.float32)
    own_residual = lax.dynamic_slice_in_dim(residual, hidden_index * local_width, local_width, 1)
    return (own_residual + mlp_piece)[None]


def solution(mesh):
    placed = (
        P(("frames", "codebook"), "hidden"),
        P("frames", "codebook"),
        P("codebook", "hidden", None),
        P("codebook", None, None),
        P("codebook", None, None, "hidden"),
        P("codebook", "hidden", None),
        P("codebook", None, None, "hidden"),
        P("codebook", "hidden", None),
        P("codebook", None, None),
    )
    return jax.shard_map(
        body,
        mesh=mesh,
        in_specs=placed,
        out_specs=P("codebook", "frames", "hidden"),
        check_vma=False,
    )
```

profile of v0, /device:TPU:1, one launch (start us, length us, event | category | flops | bytes accessed | tf_op | source)
XLA Modules:
  0.0 563.1 jit_solution(17674491881883395552)
XLA Ops:
  7.3 42.5 %all-gather.4.cloned.1.call-done = bf16[2048,1024]{1,0:T(8,128)(2,1)} async-done(((bf16[128,1024]{1,0:T(8,128)(2,1)}), bf16[2048,1024]{1,0:T(8,128)(2,1)}) %all-gather.4.cloned.1.call-update) | async-done | bytes 4194320 | tf_op jit(solution)/shard_map/all_gather | solution.py:45
  49.8 8.3 %convolution_convert_fusion.2 = bf16[2048,1024]{1,0:T(8,128)(2,1)} fusion(bf16[2048,1024]{1,0:T(8,128)(2,1)} %all-gather.4.cloned.1.call-done, bf16[1,1024,1024]{2,1,0:T(8,128)(2,1)S(1)} %copy-done), kind=kOutput, calls=%fused_computation.16 | convolution fusion | flops 4297064448 | bytes 10485760 | tf_op jit(solution)/shard_map/dot_general | solution.py:44
  58.9 2.8 collective-permute-start
  62.5 13.8 %gather_fusion = bf16[2048,1024]{1,0:T(8,128)(2,1)} fusion(bf16[2049,1024]{1,0:T(8,128)(2,1)} %bitcast.66, s32[2048]{0:T(1024)S(1)} %broadcast_clamp_fusion), kind=kCustom, calls=%fused_computation | custom fusion | bytes 8396800 | tf_op jit(solution)/shard_map/gather | solution.py:50
  76.3 74.6 %all-reduce.3.cloned.1.call-done = bf16[2048,1024]{1,0:T(8,128)(2,1)} async-done(((bf16[2048,1024]{1,0:T(8,128)(2,1)}), bf16[2048,1024]{1,0:T(8,128)(2,1)}) %all-reduce.3.cloned.1.call-update) | async-done | bytes 4194320 | tf_op jit(solution)/shard_map/psum | solution.py:50
  150.9 5.0 multiply_reduce_fusion.3
  156.0 0.9 copy-done.3
  156.8 4.2 fusion.8
  161.3 1.3 copy.21
  162.7 1.3 copy.23
  164.6 90.1 %all-gather.6.cloned.1.call-done = bf16[16,2048,256]{2,1,0:T(8,128)(2,1)} async-done(((bf16[1,2048,256]{2,1,0:T(8,128)(2,1)}), bf16[16,2048,256]{2,1,0:T(8,128)(2,1)}) %all-gather.6.cloned.1.call-update) | async-done | bytes 16777232 | tf_op jit(solution)/shard_map/all_gather | solution.py:62
  254.7 22.0 %copy.40 = bf16[16,2048,256]{1,2,0:T(8,128)(2,1)} copy(bf16[16,2048,256]{2,1,0:T(8,128)(2,1)} %all-gather.6.cloned.1.call-done) | data formatting | bytes 33554432
  276.7 7.9 %multiply_reduce_fusion.1 = f32[2048,4,16]{0,1,2:T(4,128)S(1)} fusion(f32[2048,4,64]{0,2,1:T(8,128)S(1)} %convert.1, bf16[16,2048,256]{1,2,0:T(8,128)(2,1)} %copy.40), kind=kLoop, calls=%fused_computation.2 | loop fusion | flops 25034752 | bytes 19398656
  285.8 62.8 %all-gather.8.cloned.1.call-done = bf16[16,2048,256]{2,1,0:T(8,128)(2,1)} async-done(((bf16[1,2048,256]{2,1,0:T(8,128)(2,1)}), bf16[16,2048,256]{2,1,0:T(8,128)(2,1)}) %all-gather.8.cloned.1.call-update) | async-done | bytes 16777232 | tf_op jit(solution)/shard_map/all_gather | solution.py:63
  348.6 21.7 %copy.41 = bf16[16,2048,256]{1,2,0:T(8,128)(2,1)} copy(bf16[16,2048,256]{2,1,0:T(8,128)(2,1)} %all-gather.8.cloned.1.call-done) | data formatting | bytes 33554432
  370.3 7.7 %multiply_reduce_fusion = f32[2048,4,64]{0,2,1:T(8,128)S(1)} fusion(bf16[2048,4,16,64]{0,3,1,2:T(8,128)(2,1)} %bitcast.67, f32[2048,4,16]{0,1,2:T(4,128)S(1)} %copy.43), kind=kLoop, calls=%fused_computation.1 | loop fusion | flops 24641536 | bytes 19398656 | tf_op jit(solution)/shard_map/jfh,jfhd->fhd/dot_general | solution.py:75
  378.1 3.3 convolution_convert_fusion
  381.5 93.4 %all-reduce.5.cloned.1.call-done = bf16[2048,1024]{1,0:T(8,128)(2,1)} async-done(((bf16[2048,1024]{1,0:T(8,128)(2,1)}), bf16[2048,1024]{1,0:T(8,128)(2,1)}) %all-reduce.5.cloned.1.call-update) | async-done | bytes 4194320 | tf_op jit(solution)/shard_map/psum | solution.py:84
  474.9 5.8 %multiply_reduce_fusion.2 = (f32[2048]{0:T(1024)S(1)}, f32[2048,1024]{1,0:T(8,128)S(1)}) fusion(bf16[2048,1024]{1,0:T(8,128)(2,1)} %all-reduce.5.cloned.1.call-done, bf16[2048,1024]{1,0:T(8,128)(2,1)} %gather_fusion, bf16[2048,1024]{1,0:T(8,128)(2,1)} %all-reduce.3.cloned.1.call-done), kind=kLoop, calls=%fused_computation.5 | loop fusion | flops 14678016 | bytes 20979712 | tf_op jit(solution)/shard_map/reduce_sum | solution.py:16
  480.7 3.2 copy-done.4
  483.9 6.7 %fusion.14 = f32[2048,1024]{1,0:T(8,128)} fusion(bf16[1,2,1024,1024]{3,2,1,0:T(8,128)(2,1)S(1)} %copy-done.7, f32[2048,1024]{1,0:T(8,128)S(1)} %get-tuple-element.6, f32[1024]{0:T(1024)S(1)} %bitcast.71, f32[2048]{0:T(1024)S(1)} %add_rsqrt_fusion), kind=kOutput, calls=%fused_computation.21 | convolution fusion | flops 4301258752 | bytes 18886656 | tf_op jit(solution)/shard_map/dot_general | solution.py:20
  490.6 15.1 %convolution_convert_fusion.1 = bf16[2048,1024]{1,0:T(8,128)(2,1)} fusion(f32[2048,1024]{1,0:T(8,128)} %fusion.14, bf16[1,1024,1024]{2,1,0:T(8,128)(2,1)} %param.16, bf16[1,2,1024,1024]{3,2,1,0:T(8,128)(2,1)} %param.15, f32[2048,1024]{1,0:T(8,128)} %copy-done.4, f32[1024]{0:T(1024)S(1)} %bitcast.72, f32[2048]{0:T(1024)S(1)} %add_rsqrt_fusion), kind=kOutput, calls=%fused_computation.15 | convolution fusion | flops 8610906112 | bytes 25178112 | tf_op jit(solution)/shard_map/dot_general | solution.py:87
  505.8 47.0 %reduce-scatter.2.cloned.1.call-done = bf16[2048,256]{1,0:T(8,128)(2,1)} async-done(((bf16[2048,1024]{1,0:T(8,128)(2,1)}), bf16[2048,256]{1,0:T(8,128)(2,1)}) %reduce-scatter.2.cloned.1.call-update) | async-done | bytes 1048592 | tf_op jit(solution)/shard_map/reduce_scatter | solution.py:88
  552.9 3.4 add_bitcast_fusion
  (44 shorter events, 4.6 us)
Async XLA Ops:
  6.5 43.3 %copy-start = (bf16[1,1024,1024]{2,1,0:T(8,128)(2,1)S(1)}, bf16[1,1024,1024]{2,1,0:T(8,128)(2,1)}, u32[]{:S(2)}) copy-start(bf16[1,1024,1024]{2,1,0:T(8,128)(2,1)} %param.11) | copy-start | bytes 6291460
  6.5 43.3 %all-gather.4.cloned.1.call-start = ((), (), s32[]{:S(2)}) async-start(), calls=%async_computation.1 | async-start | bytes 4456448 | tf_op jit(solution)/shard_map/all_gather | solution.py:45
  7.3 143.6 %all-reduce.3.cloned.1.call-start = ((), (), s32[]{:S(2)}) async-start(), calls=%async_computation.2 | async-start | bytes 8388608 | tf_op jit(solution)/shard_map/psum | solution.py:50
  58.2 0.7 copy-start.9
  58.2 3.5 copy-start.6
  58.2 196.5 %all-gather.6.cloned.1.call-start = ((), (), s32[]{:S(2)}) async-start(), calls=%async_computation.3 | async-start | bytes 17825792 | tf_op jit(solution)/shard_map/all_gather | solution.py:62
  58.9 3.6 collective-permute-start
  62.5 93.4 %copy-start.8 = (bf16[1,3,1024,256]{3,2,1,0:T(8,128)(2,1)S(1)}, bf16[1,3,1024,256]{3,2,1,0:T(8,128)(2,1)}, u32[]{:S(2)}) copy-start(bf16[1,3,1024,256]{3,2,1,0:T(8,128)(2,1)} %param.13) | copy-start | bytes 4718596
  150.9 5.1 copy-start.2
  150.9 5.9 %copy-start.3 = (bf16[2048,1024]{1,0:T(8,128)(2,1)S(1)}, bf16[2048,1024]{1,0:T(8,128)(2,1)}, u32[]{:S(2)}) copy-start(bf16[2048,1024]{1,0:T(8,128)(2,1)} %all-reduce.3.cloned.1.call-done) | copy-start | bytes 12582916
  162.7 185.9 %all-gather.8.cloned.1.call-start = ((), (), s32[]{:S(2)}) async-start(), calls=%async_computation.4 | async-start | bytes 17825792 | tf_op jit(solution)/shard_map/all_gather | solution.py:63
  164.1 310.8 %all-reduce.5.cloned.1.call-start = ((), (), s32[]{:S(2)}) async-start(), calls=%async_computation.5 | async-start | bytes 8388608 | tf_op jit(solution)/shard_map/psum | solution.py:84
  370.3 7.9 %copy-start.5 = (bf16[1,256,1024]{2,1,0:T(8,128)(2,1)S(1)}, bf16[1,256,1024]{2,1,0:T(8,128)(2,1)}, u32[]{:S(2)}) copy-start(bf16[1,256,1024]{2,1,0:T(8,128)(2,1)} %param.14) | copy-start | bytes 1572868
  381.4 171.4 %reduce-scatter.2.cloned.1.call-start = ((), (), s32[]{:S(2)}) async-start(), calls=%async_computation.6 | async-start | bytes 5242880 | tf_op jit(solution)/shard_map/reduce_scatter | solution.py:88
  474.9 9.1 %copy-start.7 = (bf16[1,2,1024,1024]{3,2,1,0:T(8,128)(2,1)S(1)}, bf16[1,2,1024,1024]{3,2,1,0:T(8,128)(2,1)}, u32[]{:S(2)}) copy-start(bf16[1,2,1024,1024]{3,2,1,0:T(8,128)(2,1)} %param.15) | copy-start | bytes 12582916
  480.7 3.2 copy-start.4
  505.8 50.5 %copy-start.1 = (bf16[1,1024,1024]{2,1,0:T(8,128)(2,1)S(1)}, bf16[1,1024,1024]{2,1,0:T(8,128)(2,1)}, u32[]{:S(2)}) copy-start(bf16[1,1024,1024]{2,1,0:T(8,128)(2,1)} %param.11) | copy-start | bytes 6291460
Sparse Core Ops, SparseCore 0:
  9.0 40.7 all-gather.3
  58.3 92.5 all-reduce.2
  162.8 91.8 all-gather.5
  256.2 92.3 all-gather.7
  381.6 93.2 all-reduce.4
  505.9 46.8 reduce-scatter.1
where the time goes:
time: 564 us; the launch traced here: 563 us
  waiting for transfers between devices  412 us (73%)
  local copies, waits for them, and re-layouts  65.5 us (12%)
  matrix products  37.6 us (7%)
  other arithmetic  31.1 us (6%)
  between operations  13.7 us (2%)
    psum x1, waiting for transfers between devices, body(): lax.psum(attention_part.astype(jnp.bfloat16), 'hidden').astype(jnp.float32)  93.4 us
    all_gather x1, waiting for transfers between devices, body(): key_piece = lax.all_gather(triple[1][None], 'codebook', axis=0, tiled=True)  90.1 us
    psum x1, waiting for transfers between devices, body(): lax.psum(partial_sum.astype(jnp.bfloat16), 'hidden').astype(jnp.float32)  74.6 us
    all_gather x1, waiting for transfers between devices, body(): lax.all_gather(triple[2][None], 'codebook', axis=0, tiled=True)  62.8 us
    unnamed x23, local copies, waits for them, and re-layouts  48.7 us
    reduce_scatter x1, waiting for transfers between devices, body(): lax.psum_scatter(down_part.astype(jnp.bfloat16), 'hidden', scatter_dimens...  47 us
    all_gather x1, waiting for transfers between devices, body(): lax.all_gather(temporal, 'codebook', axis=0, tiled=True)  42.5 us
    dot_general x1, matrix products, body(): jnp.dot(activated, down_weight[0], preferred_element_type=jnp.float32)  15.1 us
  transfers between devices with their start and end apart: 7, of which 7 were waited for; matrix products, arithmetic and copies ran while one was open for 8% of the time, Pallas kernels for 0%

commit v1 on v0

v1 whole, which is shorter than its diff:
```python
import functools

import jax
import jax.numpy as jnp
from jax import lax
from jax.experimental import pallas as pl
from jax.experimental.pallas import tpu as pltpu
from jax.sharding import PartitionSpec as P

HEADS = 16
MESH = pl.DeviceIdType.MESH
F32 = jnp.float32
BF16 = jnp.bfloat16
CHIPS = ((0, 1), (0, 3), (1, 0), (0, 2), (1, 1), (1, 3), (1, 2))


def kernel(
    temporal, emb_in, wp_in, wqkv_in, wo_in, wgu_in, wd_in, gains, out,
    tbuf, wp, wqkv, wo, wgu, wd, emb,
    ps2, psr, psl, pfl, pfr, prl, prr, x0,
    n1, qs, qr, att_s, att_r, bias,
    n2, act, ds2, dsr, dsl, dfl, dfr, drl, drr, oacc,
    loc, t_s, t_r, wo_s, wo_r, p_s, p_r, n_s, n_r, m_s, m_r, a_s, a_r, b_s, b_r, d_s, d_r, o_s,
):
    f = lax.axis_index("frames")
    c = lax.axis_index("codebook")
    h = lax.axis_index("hidden")
    hr, hl, ho = (h + 1) % 4, (h + 3) % 4, (h + 2) % 4
    right, left = (f, c, hr), (f, c, hl)
    y, x, k = c // 8, (c // 2) % 4, c % 2
    order = (h, hl, hr, ho)

    def rc(src, dst, ss, rs, dev):
        return pltpu.make_async_remote_copy(
            src_ref=src, dst_ref=dst, send_sem=ss, recv_sem=rs, device_id=dev, device_id_type=MESH
        )

    def got(ref, ss, rs):
        rc(ref, ref, ss, rs, right).wait_recv()

    loads = [
        pltpu.make_async_copy(s, d, loc.at[i])
        for i, (s, d) in enumerate((
            (wp_in.at[0], wp), (wqkv_in.at[0], wqkv), (wgu_in.at[0], wgu), (wd_in.at[0], wd), (emb_in, emb),
            (wo_in.at[0], wo.at[h]), (temporal, tbuf.at[pl.ds(c * 128, 128)]),
        ))
    ]
    loads[6].start()
    loads[0].start()
    for i in (4, 1, 5, 2, 3):
        loads[i].start()

    barrier = pltpu.get_barrier_semaphore()

    def greet(n, carry):
        pl.semaphore_signal(
            barrier, inc=1, device_id=(f, (c + n // 4) % 16, (h + n % 4) % 4), device_id_type=MESH
        )
        return carry

    lax.fori_loop(1, 64, greet, 0)
    pl.semaphore_wait(barrier, 63)

    loads[6].wait()
    rows_of = lambda src: tbuf.at[pl.ds(src * 128, 128)]
    partner = (f, y * 8 + x * 2 + 1 - k, h)
    sends = []
    for i, (dy, dx) in enumerate(CHIPS):
        dst = ((y + dy) % 2) * 8 + ((x + dx) % 4) * 2 + k
        sends.append(rc(rows_of(c), rows_of(c), t_s.at[i], t_r.at[c], (f, dst, h)))
    sends.append(rc(rows_of(c), rows_of(c), t_s.at[7], t_r.at[c], partner))
    for s in sends:
        s.start()
    loads[5].wait()
    for j in (1, 3, 2):
        s = rc(wo.at[h], wo.at[h], wo_s.at[j - 1], wo_r.at[h], (f, c, (h + j) % 4))
        s.start()
        sends.append(s)
    for i, (dy, dx) in enumerate(CHIPS):
        src = ((y + 2 - dy) % 2) * 8 + ((x + 4 - dx) % 4) * 2 + k
        got(rows_of(src), t_s.at[0], t_r.at[src])
        s = rc(rows_of(src), rows_of(src), t_s.at[8 + i], t_r.at[src], partner)
        s.start()
        sends.append(s)
    for i, (dy, dx) in enumerate(((0, 0),) + CHIPS):
        src = ((y + dy) % 2) * 8 + ((x + dx) % 4) * 2 + 1 - k
        got(rows_of(src), t_s.at[0], t_r.at[src])
    loads[0].wait()

    def proj(block, row0, rows, store):
        def tile(n, carry):
            cols = pl.ds(pl.multiple_of(n * 256, 256), 256)
            lhs = tbuf[pl.ds(pl.multiple_of(block * 512 + row0, 256), rows), :]
            store(cols, jnp.dot(lhs, wp[:, cols], preferred_element_type=F32))
            return carry

        lax.fori_loop(0, 4, tile, 0)

    def into(ref, row0, rows, extra=None):
        def store(cols, value):
            if extra is not None:
                value = value + extra[:, cols].astype(F32)
            ref[pl.ds(row0, rows), cols] = value.astype(ref.dtype)

        return store

    top, bot = pl.ds(0, 256), pl.ds(256, 256)

    def send(src, dst, ss, rs, dev):
        s = rc(src, dst, ss, rs, dev)
        s.start()
        sends.append(s)

    proj(ho, 0, 512, into(ps2, 0, 512))
    send(ps2.at[top], pfl, p_s.at[0], p_r.at[0], right)
    send(ps2.at[bot], pfr, p_s.at[1], p_r.at[1], left)
    proj(hr, 256, 256, into(psr, 256, 256))
    send(psr.at[bot], prl.at[bot], p_s.at[2], p_r.at[2], right)
    proj(hl, 0, 256, into(psl, 0, 256))
    send(psl.at[top], prr.at[top], p_s.at[3], p_r.at[3], left)
    loads[4].wait()
    proj(h, 0, 512, into(x0, 0, 512, emb))
    got(pfl, p_s.at[0], p_r.at[0])
    proj(hr, 0, 256, into(psr, 0, 256, pfl))
    send(psr.at[top], prl.at[top], p_s.at[4], p_r.at[4], right)
    got(pfr, p_s.at[1], p_r.at[1])
    proj(hl, 256, 256, into(psl, 256, 256, pfr))
    send(psl.at[bot], prr.at[bot], p_s.at[5], p_r.at[5], left)
    for i, ref in ((2, prl.at[bot]), (3, prr.at[top]), (4, prl.at[top]), (5, prr.at[bot])):
        got(ref, p_s.at[i], p_r.at[i])

    def norm_rows(dst, gain, extras):
        def chunk(n, carry):
            rows = pl.ds(pl.multiple_of(n * 32, 32), 32)
            v = x0[rows, :]
            for e in extras:
                v = v + e[rows, :].astype(F32)
            if extras:
                x0[rows, :] = v
            scale = lax.rsqrt(jnp.mean(v * v, axis=-1, keepdims=True) + 1e-05)
            dst[h, rows, :] = (v * scale * gain).astype(BF16)
            return carry

        lax.fori_loop(0, 16, chunk, 0)

    norm_rows(n1, gains[0, 0:1, :], (prl, prr))

    def ag_start(buf, ss, rs):
        send(buf.at[h, top], buf.at[h, top], ss.at[0], rs.at[0], right)
        send(buf.at[h, bot], buf.at[h, bot], ss.at[2], rs.at[2], left)
        send(buf.at[h, bot], buf.at[h, bot], ss.at[1], rs.at[1], right)
        send(buf.at[h, top], buf.at[h, top], ss.at[3], rs.at[3], left)

    def ag_forward(buf, ss, rs):
        got(buf.at[hl, top], ss.at[0], rs.at[0])
        send(buf.at[hl, top], buf.at[hl, top], ss.at[4], rs.at[4], right)
        got(buf.at[hr, bot], ss.at[2], rs.at[2])
        send(buf.at[hr, bot], buf.at[hr, bot], ss.at[5], rs.at[5], left)

    def ag_wait(buf, ss, rs, pos):
        if pos == 1:
            got(buf.at[hl, bot], ss.at[1], rs.at[1])
        if pos == 2:
            got(buf.at[hr, top], ss.at[3], rs.at[3])
        if pos == 3:
            got(buf.at[ho, top], ss.at[4], rs.at[4])
            got(buf.at[ho, bot], ss.at[5], rs.at[5])

    ag_start(n1, n_s, n_r)

    row = lax.broadcasted_iota(jnp.int32, (256, 256), 0)
    col = lax.broadcasted_iota(jnp.int32, (256, 256), 1)
    seen = (row % 16 == col % 16) & (row // 16 >= col // 16)
    bias[...] = jnp.where(seen, 0.0, -1e30)
    loads[1].wait()

    def qkv(r):
        for i in range(3):
            part = jnp.dot(n1[r], wqkv[i], preferred_element_type=F32)
            qs[r, :, i * 256:(i + 1) * 256] = part.astype(BF16)

        def post(d, carry):
            dst = ((y + d // 8) % 2) * 8 + ((x + (d // 2) % 4) % 4) * 2 + (k + d) % 2
            rc(
                qs.at[r, pl.ds(dst * 32, 32)], qr.at[r, c], a_s.at[r, dst], a_r.at[r, c], (f, dst, h)
            ).start()
            return carry

        lax.fori_loop(1, 16, post, 0)
        qr[r, c] = qs[r, pl.ds(pl.multiple_of(c * 32, 32), 32), :]

    def attend(r):
        def arrived(d, carry):
            src = (c + d) % 16
            got(qr.at[r, src], a_s.at[r, 0], a_r.at[r, src])
            return carry

        lax.fori_loop(1, 16, arrived, 0)

        def unit(n, carry):
            frames = pl.ds(pl.multiple_of((n // 2) * 16, 16), 16)
            pair = (n % 2) * 128
            take = lambda i: qr[
                r, :, frames, pl.ds(pl.multiple_of(i * 256 + pair, 128), 128)
            ].reshape(256, 128)
            q, kk, v = take(0), take(1), take(2)
            lane = lax.broadcasted_iota(jnp.int32, (256, 128), 1)
            halves = []
            for half in range(2):
                mine = (lane // 64) == half
                qh = jnp.where(mine, q, jnp.zeros_like(q))
                parts = []
                for rows, width in ((slice(0, 128), 128), (slice(128, 256), 256)):
                    s = lax.dot_general(
                        qh[rows], kk[:width], (((1,), (1,)), ((), ())), preferred_element_type=F32
                    )
                    s = s * 0.125 + bias[rows, :width]
                    e = jnp.exp(s - jnp.max(s, axis=-1, keepdims=True))
                    total = jnp.sum(e, axis=-1, keepdims=True)
                    o = jnp.dot(e.astype(BF16), v[:width], preferred_element_type=F32)
                    parts.append(o / total)
                halves.append(jnp.concatenate(parts, axis=0))
            o = jnp.where((lane // 64) == 0, halves[0], halves[1]).astype(BF16)
            att_s[r, :, frames, pl.ds(pl.multiple_of(pair, 128), 128)] = o.reshape(16, 16, 128)
            return carry

        lax.fori_loop(0, 4, unit, 0)

        def post(d, carry):
            dst = ((y + d // 8) % 2) * 8 + ((x + (d // 2) % 4) % 4) * 2 + (k + d) % 2
            rc(
                att_s.at[r, dst], att_r.at[h, pl.ds(c * 32, 32)], b_s.at[r, dst], b_r.at[h, c], (f, dst, r)
            ).start()
            return carry

        return post

    def attend_own():
        lax.fori_loop(1, 16, attend(h), 0)
        att_r[h, pl.ds(pl.multiple_of(c * 32, 32), 32), :] = att_s[h, c]

    qkv(h)
    ag_forward(n1, n_s, n_r)
    attend_own()
    ag_wait(n1, n_s, n_r, 1)
    qkv(hl)
    ag_wait(n1, n_s, n_r, 2)
    qkv(hr)
    lax.fori_loop(0, 16, attend(hl), 0)
    lax.fori_loop(0, 16, attend(hr), 0)
    ag_wait(n1, n_s, n_r, 3)
    qkv(ho)
    lax.fori_loop(0, 16, attend(ho), 0)

    def out_part(src):
        def tile(n, carry):
            cols = pl.ds(pl.multiple_of(n * 256, 256), 256)
            x0[:, cols] += jnp.dot(att_r[src], wo[src, :, cols], preferred_element_type=F32)
            return carry

        lax.fori_loop(0, 4, tile, 0)

    for pos, src in enumerate(order):
        if pos:
            got(wo.at[src], wo_s.at[0], wo_r.at[src])

        def arrived(d, carry):
            at = (c + d) % 16
            got(att_r.at[src, pl.ds(at * 32, 32)], b_s.at[0, 0], b_r.at[src, at])
            return carry

        lax.fori_loop(0 if pos else 1, 16, arrived, 0)
        out_part(src)

    norm_rows(n2, gains[0, 1:2, :], ())
    ag_start(n2, m_s, m_r)
    loads[2].wait()
    loads[3].wait()

    def down(pos, row0, rows, target):
        return jnp.dot(
            act[pos, pl.ds(row0, rows), :],
            wd[:, pl.ds(pl.multiple_of(target * 256, 256), 256)],
            preferred_element_type=F32,
        )

    def mine(pos, row0, rows, target):
        value = down(pos, row0, rows, target)
        if pos == 0:
            value = value + x0[pl.ds(row0, rows), pl.ds(pl.multiple_of(target * 256, 256), 256)]
        return value

    def mlp(pos):
        r = order[pos]

        def tile(n, carry):
            cols = pl.ds(pl.multiple_of(n * 256, 256), 256)
            g = jnp.dot(n2[r], wgu[0, :, cols], preferred_element_type=F32)
            u = jnp.dot(n2[r], wgu[1, :, cols], preferred_element_type=F32)
            act[pos, :, cols] = (g / (1.0 + jnp.exp(-g)) * u).astype(BF16)
            return carry

        lax.fori_loop(0, 4, tile, 0)
        ds2[pos] = mine(pos, 0, 512, ho).astype(BF16)
        send(ds2.at[pos, top], dfl.at[r], d_s.at[pos, 0], d_r.at[r, 0], right)
        send(ds2.at[pos, bot], dfr.at[r], d_s.at[pos, 1], d_r.at[r, 1], left)
        dsr[pos, bot, :] = mine(pos, 256, 256, hr).astype(BF16)
        send(dsr.at[pos, bot], drl.at[r, bot], d_s.at[pos, 2], d_r.at[r, 2], right)
        dsl[pos, top, :] = mine(pos, 0, 256, hl).astype(BF16)
        send(dsl.at[pos, top], drr.at[r, top], d_s.at[pos, 3], d_r.at[r, 3], left)
        oacc[pos] = mine(pos, 0, 512, h)

    def pass_right(pos):
        r = order[pos]
        got(dfl.at[r], d_s.at[pos, 0], d_r.at[r, 0])
        dsr[pos, top, :] = (mine(pos, 0, 256, hr) + dfl[r].astype(F32)).astype(BF16)
        send(dsr.at[pos, top], drl.at[r, top], d_s.at[pos, 4], d_r.at[r, 4], right)

    def pass_left(pos):
        r = order[pos]
        got(dfr.at[r], d_s.at[pos, 1], d_r.at[r, 1])
        dsl[pos, bot, :] = (mine(pos, 256, 256, hl) + dfr[r].astype(F32)).astype(BF16)
        send(dsl.at[pos, bot], drr.at[r, bot], d_s.at[pos, 5], d_r.at[r, 5], left)

    mlp(0)
    ag_forward(n2, m_s, m_r)
    ag_wait(n2, m_s, m_r, 1)
    mlp(1)
    ag_wait(n2, m_s, m_r, 2)
    mlp(2)
    pass_right(1)
    pass_left(2)
    ag_wait(n2, m_s, m_r, 3)
    mlp(3)
    pass_right(3)
    pass_left(0)
    pass_right(0)
    pass_left(3)
    pass_right(2)
    pass_left(1)

    writes = []
    for pos in (1, 2, 0, 3):
        r = order[pos]
        for i, ref in ((2, drl.at[r, bot]), (3, drr.at[r, top]), (4, drl.at[r, top]), (5, drr.at[r, bot])):
            got(ref, d_s.at[pos, i], d_r.at[r, i])
        oacc[pos] = oacc[pos] + drl[r].astype(F32) + drr[r].astype(F32)
        w = pltpu.make_async_copy(oacc.at[pos], out.at[r], o_s.at[pos])
        w.start()
        writes.append(w)

    for s in sends:
        s.wait_send()

    def sent(d, carry):
        for r in range(4):
            at = (c + d) % 16
            rc(qs.at[r, pl.ds(at * 32, 32)], qr.at[r, c], a_s.at[r, at], a_r.at[r, c], right).wait_send()
        return carry

    lax.fori_loop(1, 16, sent, 0)

    def returned(d, carry):
        for j in range(1, 4):
            r = (h + j) % 4
            rc(att_s.at[r, d], att_r.at[h, pl.ds(c * 32, 32)], b_s.at[r, d], b_r.at[h, c], right).wait_send()
        return carry

    lax.fori_loop(0, 16, returned, 0)

    def returned_own(d, carry):
        at = (c + d) % 16
        rc(att_s.at[h, at], att_r.at[h, pl.ds(c * 32, 32)], b_s.at[h, at], b_r.at[h, c], right).wait_send()
        return carry

    lax.fori_loop(1, 16, returned_own, 0)
    for w in writes:
        w.wait()


def body(temporal, frame_ids, proj_weight, embed_table, qkv_weight, out_weight, gate_up, down_weight, norm_gains):
    c = lax.axis_index("codebook")
    h = lax.axis_index("hidden")
    start_id = embed_table.shape[1] - 1
    own_ids = lax.dynamic_slice_in_dim(frame_ids[:, 0], h * 512, 512, 0)
    earlier = lax.ppermute(own_ids, "codebook", [(i, i + 1) for i in range(15)])
    previous = jnp.where(c == 0, start_id, earlier)
    emb = embed_table[0][previous]
    vm, dma = pltpu.VMEM, pltpu.SemaphoreType.DMA
    any_spec = pl.BlockSpec(memory_space=pl.ANY)
    result = pl.pallas_call(
        kernel,
        name="depth_layer",
        out_shape=jax.ShapeDtypeStruct((4, 512, 256), F32),
        in_specs=[any_spec] * 7 + [pl.BlockSpec(memory_space=pltpu.VMEM)],
        out_specs=any_spec,
        scratch_shapes=[
            vm((2048, 1024), BF16), vm((1024, 1024), BF16), vm((3, 1024, 256), BF16), vm((4, 256, 1024), BF16),
            vm((2, 1024, 1024), BF16), vm((1024, 1024), BF16), vm((512, 1024), BF16),
            vm((512, 1024), BF16), vm((512, 1024), BF16), vm((512, 1024), BF16),
            vm((256, 1024), BF16), vm((256, 1024), BF16), vm((512, 1024), BF16), vm((512, 1024), BF16),
            vm((512, 1024), F32),
            vm((4, 512, 1024), BF16), vm((4, 512, 768), BF16), vm((4, 16, 32, 768), BF16),
            vm((4, 16, 32, 256), BF16), vm((4, 512, 256), BF16), vm((256, 256), F32),
            vm((4, 512, 1024), BF16), vm((4, 512, 1024), BF16),
            vm((4, 512, 256), BF16), vm((4, 512, 256), BF16), vm((4, 512, 256), BF16),
            vm((4, 256, 256), BF16), vm((4, 256, 256), BF16), vm((4, 512, 256), BF16), vm((4, 512, 256), BF16),
            vm((4, 512, 256), F32),
            dma((7,)), dma((15,)), dma((16,)), dma((3,)), dma((4,)), dma((6,)), dma((6,)),
            dma((6,)), dma((6,)), dma((6,)), dma((6,)), dma((4, 16)), dma((4, 16)), dma((4, 16)), dma((4, 16)),
            dma((4, 6)), dma((4, 6)), dma((4,)),
        ],
        compiler_params=pltpu.CompilerParams(
            collective_id=0, has_side_effects=True, vmem_limit_bytes=67043328
        ),
    )(temporal, emb, proj_weight, qkv_weight, out_weight, gate_up, down_weight, norm_gains)
    return result.reshape(1, 2048, 256)


def solution(mesh):
    placed = (
        P(("frames", "codebook"), "hidden"),
        P("frames", "codebook"),
        P("codebook", "hidden", None),
        P("codebook", None, None),
        P("codebook", None, None, "hidden"),
        P("codebook", "hidden", None),
        P("codebook", None, None, "hidden"),
        P("codebook", "hidden", None),
        P("codebook", None, None),
    )
    return jax.shard_map(
        body,
        mesh=mesh,
        in_specs=placed,
        out_specs=P("codebook", "frames", "hidden"),
        check_vma=False,
    )
```

time: 564 us -> 251 us (0.45)
  waiting for transfers between devices: 412 us -> 0.71 us
  Pallas kernels: 0 us -> 236 us
  local copies, waits for them, and re-layouts: 65.5 us -> 9.93 us
  matrix products: 37.6 us -> 0 us
  other arithmetic: 31.1 us -> 0.01 us
  between operations: 13.7 us -> 0.03 us
    pallas_call x0 -> x1, Pallas kernels: none -> 236 us  [body(): pl.pallas_call(kernel, name='depth_layer', out_shape=jax.ShapeDtypeStruct...]
    all_gather x3 -> x0, waiting for transfers between devices: 195 us -> none  [the longest x1 90.1 us: body(): key_piece = lax.all_gather(triple[1][None], 'codebook', axis=0, tiled=True)]
    psum x2 -> x0, waiting for transfers between devices: 168 us -> none  [the longest x1 93.4 us: body(): lax.psum(attention_part.astype(jnp.bfloat16), 'hidden').astype(jnp.float32)]
    reduce_scatter x1 -> x0, waiting for transfers between devices: 47 us -> none  [body(): lax.psum_scatter(down_part.astype(jnp.bfloat16), 'hidden', scatter_dimens...]
    unnamed x23 -> x1, local copies, waits for them, and re-layouts: 48.7 us -> 3.05 us
    dot_general x5 -> x0, matrix products: 37.6 us -> none  [the longest x1 15.1 us: body(): jnp.dot(activated, down_weight[0], preferred_element_type=jnp.float32)]
    reduce_sum x3 -> x0, other arithmetic: 11.3 us -> none  [the longest x2 10.9 us: normalize(): jnp.mean(values * values, axis=-1, keepdims=True) + 1e-05]
    unnamed x2 -> x0, other arithmetic: 8.09 us -> none
  transfers between devices with their start and end apart: 7 -> 1, of which waited for: 7 -> 1; matrix products, arithmetic and copies ran while one was open for 8% -> 0% of each run, Pallas kernels for 0% -> 0%
where the time goes in v1:
time: 251 us
  Pallas kernels  236 us (94%)
  local copies, waits for them, and re-layouts  9.93 us (4%)
  starting transfers between devices  4.49 us (2%)
    pallas_call x1, Pallas kernels, body(): pl.pallas_call(kernel, name='depth_layer', out_shape=jax.ShapeDtypeStruct...  236 us
    gather x1, local copies, waits for them, and re-layouts, body(): emb = embed_table[0][previous]  6.2 us
  transfers between devices with their start and end apart: 1, of which 1 were waited for; matrix products, arithmetic and copies ran while one was open for 0% of the time, Pallas kernels for 0%

profile of v1, /device:TPU:1, one launch (start us, length us, event | category | flops | bytes accessed | tf_op | source)
XLA Modules:
  0.0 250.9 jit_solution(6113271526593601983)
XLA Ops:
  0.0 0.7 constant_dynamic-slice_fusion
  0.7 4.5 %collective-permute-start = (s32[512]{0:T(512)S(1)}, s32[512]{0:T(512)S(1)}, u32[]{:S(2)}, u32[]{:S(2)}) collective-permute-start(s32[512]{0:T(512)S(1)} %bitcast.5), channel_id=1, source_target_pairs={{0,4},{4,8},{8,12},{12,16},{16,20},{20,24},{24,28},{28,32},{32,36}... | collective-permute-start | bytes 6152 | tf_op jit(solution)/shard_map/ppermute | solution.py:386
  5.2 0.7 collective-permute-done
  5.9 6.2 %gather_fusion = bf16[512,1024]{1,0:T(8,128)(2,1)} fusion(bf16[2049,1024]{1,0:T(8,128)(2,1)} %bitcast.3, s32[1024]{0:T(1024)S(1)} %pad_clamp_fusion), kind=kCustom, calls=%fused_computation | custom fusion | bytes 2099200 | tf_op jit(solution)/shard_map/gather | solution.py:388
  12.1 235.8 %depth_layer.1 = f32[4,512,256]{2,1,0:T(8,128)} custom-call(bf16[128,1024]{1,0:T(8,128)(2,1)} %temporal.1, bf16[512,1024]{1,0:T(8,128)(2,1)} %gather_fusion, bf16[1,1024,1024]{2,1,0:T(8,128)(2,1)} %wp_in.1, bf16[1,3,1024,256]{3,2,1,0:T(8,128)(2,1)} %wqkv_in.1, bf16[1,256,1024]{2,1,0:T(8,128)(2,1)} %wo_in.1, bf16[1,2,1024,1024]{3,2,1,0:T(8,128)(2,1)} %wgu_in.1, ...), custom_call_target="tpu_custom_call" | custom-call | tf_op jit(solution)/shard_map/depth_layer/pallas_call | solution.py:391
  247.9 3.0 %copy.11 = f32[1,2048,256]{2,1,0:T(8,128)} copy(f32[1,2048,256]{2,1,0:T(8,128)} %bitcast.4) | data formatting | bytes 4194304
  (2 shorter events, 0.0 us)
Async XLA Ops:
  0.7 5.2 %collective-permute-start = (s32[512]{0:T(512)S(1)}, s32[512]{0:T(512)S(1)}, u32[]{:S(2)}, u32[]{:S(2)}) collective-permute-start(s32[512]{0:T(512)S(1)} %bitcast.5), channel_id=1, source_target_pairs={{0,4},{4,8},{8,12},{12,16},{16,20},{20,24},{24,28},{28,32},{32,36}... | collective-permute-start | bytes 6152 | tf_op jit(solution)/shard_map/ppermute | solution.py:386

commit v2 on v1

v2 whole, which is shorter than its diff:
```python
import functools

import jax
import jax.numpy as jnp
from jax import lax
from jax.experimental import pallas as pl
from jax.experimental.pallas import tpu as pltpu
from jax.sharding import PartitionSpec as P

HEADS = 16
MESH = pl.DeviceIdType.MESH
F32 = jnp.float32
BF16 = jnp.bfloat16
CHIPS = ((0, 1), (0, 3), (1, 0), (0, 2), (1, 1), (1, 3), (1, 2))


def kernel(
    temporal, emb_in, wp_in, wqkv_in, wo_in, wgu_in, wd_in, gains, out,
    tbuf, wp, wqkv, wo, wgu, wd, emb,
    ps2, psr, psl, pfl, pfr, prl, prr, x0,
    n1, qs, qr, att_s, att_r, bias,
    n2, act, ds2, dsr, dsl, dfl, dfr, drl, drr, oacc,
    loc, t_s, t_r, wo_s, wo_r, p_s, p_r, n_s, n_r, m_s, m_r, a_s, a_r, b_s, b_r, d_s, d_r, o_s,
):
    f = lax.axis_index("frames")
    c = lax.axis_index("codebook")
    h = lax.axis_index("hidden")
    hr, hl, ho = (h + 1) % 4, (h + 3) % 4, (h + 2) % 4
    right, left = (f, c, hr), (f, c, hl)
    y, x, k = c // 8, (c // 2) % 4, c % 2
    order = (h, hl, hr, ho)
    top, bot = pl.ds(0, 128), pl.ds(128, 128)
    sends = []

    def rc(src, dst, ss, rs, dev):
        return pltpu.make_async_remote_copy(
            src_ref=src, dst_ref=dst, send_sem=ss, recv_sem=rs, device_id=dev, device_id_type=MESH
        )

    def send(src, dst, ss, rs, dev):
        s = rc(src, dst, ss, rs, dev)
        s.start()
        sends.append(s)

    def got(ref, ss, rs):
        rc(ref, ref, ss, rs, right).wait_recv()

    loads = [
        pltpu.make_async_copy(s, d, loc.at[i])
        for i, (s, d) in enumerate((
            (wp_in.at[0], wp), (wqkv_in.at[0], wqkv), (wgu_in.at[0], wgu), (wd_in.at[0], wd), (emb_in, emb),
            (wo_in.at[0], wo.at[h]), (temporal.at[0], tbuf.at[0, c]), (temporal.at[1], tbuf.at[1, c]),
        ))
    ]
    for i in (6, 7, 0, 4, 5, 1, 2, 3):
        loads[i].start()

    barrier = pltpu.get_barrier_semaphore()

    def greet(n, carry):
        pl.semaphore_signal(
            barrier, inc=1, device_id=(f, (c + n // 4) % 16, (h + n % 4) % 4), device_id_type=MESH
        )
        return carry

    lax.fori_loop(1, 64, greet, 0)
    pl.semaphore_wait(barrier, 63)

    partner = (f, y * 8 + x * 2 + 1 - k, h)

    def temporal_out(q):
        loads[6 + q].wait()
        for i, (dy, dx) in enumerate(CHIPS):
            dst = ((y + dy) % 2) * 8 + ((x + dx) % 4) * 2 + k
            send(tbuf.at[q, c], tbuf.at[q, c], t_s.at[q, i], t_r.at[q, c], (f, dst, h))
        send(tbuf.at[q, c], tbuf.at[q, c], t_s.at[q, 7], t_r.at[q, c], partner)

    def temporal_in(q):
        for i, (dy, dx) in enumerate(CHIPS):
            src = ((y + 2 - dy) % 2) * 8 + ((x + 4 - dx) % 4) * 2 + k
            got(tbuf.at[q, src], t_s.at[q, 0], t_r.at[q, src])
            send(tbuf.at[q, src], tbuf.at[q, src], t_s.at[q, 8 + i], t_r.at[q, src], partner)
        for dy, dx in ((0, 0),) + CHIPS:
            src = ((y + dy) % 2) * 8 + ((x + dx) % 4) * 2 + 1 - k
            got(tbuf.at[q, src], t_s.at[q, 0], t_r.at[q, src])

    def proj(q, block, row0, rows, store):
        def tile(n, carry):
            cols = pl.ds(pl.multiple_of(n * 256, 256), 256)
            lhs = tbuf[q, pl.ds(block * 4 + row0 // 64, rows // 64)].reshape(rows, 1024)
            store(cols, jnp.dot(lhs, wp[:, cols], preferred_element_type=F32))
            return carry

        lax.fori_loop(0, 4, tile, 0)

    def into(ref, row0, rows, extra=None):
        def store(cols, value):
            if extra is not None:
                value = value + extra[:, cols].astype(F32)
            ref[pl.ds(row0, rows), cols] = value.astype(ref.dtype)

        return store

    def proj_far(q):
        ss, rs = p_s.at[q], p_r.at[q]
        proj(q, ho, 0, 256, into(ps2.at[q], 0, 256))
        send(ps2.at[q, top], pfl.at[q], ss.at[0], rs.at[0], right)
        send(ps2.at[q, bot], pfr.at[q], ss.at[1], rs.at[1], left)

    def proj_near(q):
        ss, rs = p_s.at[q], p_r.at[q]
        proj(q, hr, 128, 128, into(psr.at[q], 128, 128))
        send(psr.at[q, bot], prl.at[q, bot], ss.at[2], rs.at[2], right)
        proj(q, hl, 0, 128, into(psl.at[q], 0, 128))
        send(psl.at[q, top], prr.at[q, top], ss.at[3], rs.at[3], left)

    def proj_own(q):
        proj(q, h, 0, 256, into(x0.at[q], 0, 256, emb.at[q]))

    def proj_pass(q):
        ss, rs = p_s.at[q], p_r.at[q]
        got(pfl.at[q], ss.at[0], rs.at[0])
        proj(q, hr, 0, 128, into(psr.at[q], 0, 128, pfl.at[q]))
        send(psr.at[q, top], prl.at[q, top], ss.at[4], rs.at[4], right)
        got(pfr.at[q], ss.at[1], rs.at[1])
        proj(q, hl, 128, 128, into(psl.at[q], 128, 128, pfr.at[q]))
        send(psl.at[q, bot], prr.at[q, bot], ss.at[5], rs.at[5], left)

    def norm_rows(q, dst, gain, extras):
        def chunk(n, carry):
            rows = pl.ds(pl.multiple_of(n * 32, 32), 32)
            v = x0[q, rows, :]
            for e in extras:
                v = v + e[q, rows, :].astype(F32)
            if extras:
                x0[q, rows, :] = v
            scale = lax.rsqrt(jnp.mean(v * v, axis=-1, keepdims=True) + 1e-05)
            dst[q, h, rows, :] = (v * scale * gain).astype(BF16)
            return carry

        lax.fori_loop(0, 8, chunk, 0)

    def norm_one(q):
        for i, ref in ((2, prl.at[q, bot]), (3, prr.at[q, top]), (4, prl.at[q, top]), (5, prr.at[q, bot])):
            got(ref, p_s.at[q, i], p_r.at[q, i])
        norm_rows(q, n1, gains[0, 0:1, :], (prl, prr))

    def ag_start(buf, ss, rs):
        send(buf.at[h, top], buf.at[h, top], ss.at[0], rs.at[0], right)
        send(buf.at[h, bot], buf.at[h, bot], ss.at[2], rs.at[2], left)
        send(buf.at[h, bot], buf.at[h, bot], ss.at[1], rs.at[1], right)
        send(buf.at[h, top], buf.at[h, top], ss.at[3], rs.at[3], left)

    def ag_forward(buf, ss, rs):
        got(buf.at[hl, top], ss.at[0], rs.at[0])
        send(buf.at[hl, top], buf.at[hl, top], ss.at[4], rs.at[4], right)
        got(buf.at[hr, bot], ss.at[2], rs.at[2])
        send(buf.at[hr, bot], buf.at[hr, bot], ss.at[5], rs.at[5], left)

    def ag_wait(buf, ss, rs, pos):
        if pos == 1:
            got(buf.at[hl, bot], ss.at[1], rs.at[1])
        if pos == 2:
            got(buf.at[hr, top], ss.at[3], rs.at[3])
        if pos == 3:
            got(buf.at[ho, top], ss.at[4], rs.at[4])
            got(buf.at[ho, bot], ss.at[5], rs.at[5])

    ag_one = lambda q: (n1.at[q], n_s.at[q], n_r.at[q])
    ag_two = lambda q: (n2.at[q], m_s.at[q], m_r.at[q])

    def peer(d):
        return ((y + d // 8) % 2) * 8 + ((x + (d // 2) % 4) % 4) * 2 + (k + d) % 2

    def qkv(q, pos):
        r = order[pos]
        ag_wait(*ag_one(q), pos)
        for i in range(3):
            part = jnp.dot(n1[q, r], wqkv[i], preferred_element_type=F32)
            qs[q, r, :, i * 256:(i + 1) * 256] = part.astype(BF16)

        def post(d, carry):
            dst = peer(d)
            rc(
                qs.at[q, r, pl.ds(dst * 16, 16)], qr.at[q, r, c], a_s.at[q, r], a_r.at[q, r], (f, dst, h)
            ).start()
            return carry

        lax.fori_loop(1, 16, post, 0)
        qr[q, r, c] = qs[q, r, pl.ds(pl.multiple_of(c * 16, 16), 16), :]

    def attend(q, pos):
        r = order[pos]
        got(qr.at[q, r, pl.ds(0, 15)], a_s.at[q, r], a_r.at[q, r])

        def unit(n, carry):
            pair = n * 128
            take = lambda i: qr[
                q, r, :, :, pl.ds(pl.multiple_of(i * 256 + pair, 128), 128)
            ].reshape(256, 128)
            qq, kk, v = take(0), take(1), take(2)
            lane = lax.broadcasted_iota(jnp.int32, (256, 128), 1)
            halves = []
            for half in range(2):
                mine = (lane // 64) == half
                qh = jnp.where(mine, qq, jnp.zeros_like(qq))
                parts = []
                for rows, width in ((slice(0, 128), 128), (slice(128, 256), 256)):
                    s = lax.dot_general(
                        qh[rows], kk[:width], (((1,), (1,)), ((), ())), preferred_element_type=F32
                    )
                    s = s * 0.125 + bias[rows, :width]
                    e = jnp.exp(s - jnp.max(s, axis=-1, keepdims=True))
                    total = jnp.sum(e, axis=-1, keepdims=True)
                    o = jnp.dot(e.astype(BF16), v[:width], preferred_element_type=F32)
                    parts.append(o / total)
                halves.append(jnp.concatenate(parts, axis=0))
            o = jnp.where((lane // 64) == 0, halves[0], halves[1]).astype(BF16)
            att_s[q, r, :, :, pl.ds(pl.multiple_of(pair, 128), 128)] = o.reshape(16, 16, 128)
            return carry

        lax.fori_loop(0, 2, unit, 0)

        def post(d, carry):
            dst = peer(d)
            rc(
                att_s.at[q, r, dst], att_r.at[q, h, pl.ds(c * 16, 16)], b_s.at[q, r], b_r.at[q, h], (f, dst, r)
            ).start()
            return carry

        lax.fori_loop(0 if pos else 1, 16, post, 0)
        if pos == 0:
            att_r[q, h, pl.ds(pl.multiple_of(c * 16, 16), 16), :] = att_s[q, h, c]

    def out_proj(q):
        for pos, src in enumerate(order):
            got(att_r.at[q, src, pl.ds(0, 256 if pos else 240)], b_s.at[q, src], b_r.at[q, src])

        def tile(n, carry):
            cols = pl.ds(pl.multiple_of(n * 256, 256), 256)
            total = x0[q, :, cols]
            for src in range(4):
                total = total + jnp.dot(att_r[q, src], wo[src, :, cols], preferred_element_type=F32)
            x0[q, :, cols] = total
            return carry

        lax.fori_loop(0, 4, tile, 0)
        norm_rows(q, n2, gains[0, 1:2, :], ())
        ag_start(*ag_two(q))

    def mine(q, pos, row0, rows, target):
        cols = pl.ds(pl.multiple_of(target * 256, 256), 256)
        value = jnp.dot(act[q, pos, pl.ds(row0, rows), :], wd[:, cols], preferred_element_type=F32)
        if pos == 0:
            value = value + x0[q, pl.ds(row0, rows), cols]
        return value

    def mlp(q, pos):
        r = order[pos]
        ss, rs = d_s.at[q, pos], d_r.at[q, r]
        ag_wait(*ag_two(q), pos)

        def tile(n, carry):
            cols = pl.ds(pl.multiple_of(n * 256, 256), 256)
            g = jnp.dot(n2[q, r], wgu[0, :, cols], preferred_element_type=F32)
            u = jnp.dot(n2[q, r], wgu[1, :, cols], preferred_element_type=F32)
            act[q, pos, :, cols] = (g / (1.0 + jnp.exp(-g)) * u).astype(BF16)
            return carry

        lax.fori_loop(0, 4, tile, 0)
        ds2[q, pos] = mine(q, pos, 0, 256, ho).astype(BF16)
        send(ds2.at[q, pos, top], dfl.at[q, r], ss.at[0], rs.at[0], right)
        send(ds2.at[q, pos, bot], dfr.at[q, r], ss.at[1], rs.at[1], left)
        dsr[q, pos, bot, :] = mine(q, pos, 128, 128, hr).astype(BF16)
        send(dsr.at[q, pos, bot], drl.at[q, r, bot], ss.at[2], rs.at[2], right)
        dsl[q, pos, top, :] = mine(q, pos, 0, 128, hl).astype(BF16)
        send(dsl.at[q, pos, top], drr.at[q, r, top], ss.at[3], rs.at[3], left)
        oacc[q, pos] = mine(q, pos, 0, 256, h).reshape(4, 64, 256)

    def pass_right(q, pos):
        r = order[pos]
        ss, rs = d_s.at[q, pos], d_r.at[q, r]
        got(dfl.at[q, r], ss.at[0], rs.at[0])
        dsr[q, pos, top, :] = (mine(q, pos, 0, 128, hr) + dfl[q, r].astype(F32)).astype(BF16)
        send(dsr.at[q, pos, top], drl.at[q, r, top], ss.at[4], rs.at[4], right)

    def pass_left(q, pos):
        r = order[pos]
        ss, rs = d_s.at[q, pos], d_r.at[q, r]
        got(dfr.at[q, r], ss.at[1], rs.at[1])
        dsl[q, pos, bot, :] = (mine(q, pos, 128, 128, hl) + dfr[q, r].astype(F32)).astype(BF16)
        send(dsl.at[q, pos, bot], drr.at[q, r, bot], ss.at[5], rs.at[5], left)

    writes = []

    def finish(q, pos):
        r = order[pos]
        for i, ref in (
            (2, drl.at[q, r, bot]), (3, drr.at[q, r, top]), (4, drl.at[q, r, top]), (5, drr.at[q, r, bot])
        ):
            got(ref, d_s.at[q, pos, i], d_r.at[q, r, i])
        gathered = drl[q, r].astype(F32) + drr[q, r].astype(F32)
        oacc[q, pos] = oacc[q, pos] + gathered.reshape(4, 64, 256)
        w = pltpu.make_async_copy(oacc.at[q, pos], out.at[r, :, q], o_s.at[q, pos])
        w.start()
        writes.append(w)

    temporal_out(0)
    temporal_out(1)
    loads[5].wait()
    for j in (1, 3, 2):
        send(wo.at[h], wo.at[h], wo_s.at[j - 1], wo_r.at[h], (f, c, (h + j) % 4))
    row = lax.broadcasted_iota(jnp.int32, (256, 256), 0)
    col = lax.broadcasted_iota(jnp.int32, (256, 256), 1)
    bias[...] = jnp.where((row % 16 == col % 16) & (row // 16 >= col // 16), 0.0, -1e30)
    loads[0].wait()
    temporal_in(0)
    proj_far(0)
    proj_near(0)
    loads[4].wait()
    proj_own(0)
    proj_pass(0)
    temporal_in(1)
    proj_far(1)
    norm_one(0)
    ag_start(*ag_one(0))
    loads[1].wait()
    qkv(0, 0)
    proj_near(1)
    proj_own(1)
    ag_forward(*ag_one(0))
    proj_pass(1)
    attend(0, 0)
    qkv(0, 1)
    qkv(0, 2)
    qkv(0, 3)
    attend(0, 1)
    attend(0, 2)
    norm_one(1)
    ag_start(*ag_one(1))
    qkv(1, 0)
    attend(0, 3)
    for src in order[1:]:
        got(wo.at[src], wo_s.at[0], wo_r.at[src])
    out_proj(0)
    ag_forward(*ag_one(1))
    loads[2].wait()
    loads[3].wait()
    mlp(0, 0)
    attend(1, 0)
    qkv(1, 1)
    qkv(1, 2)
    ag_forward(*ag_two(0))
    qkv(1, 3)
    attend(1, 1)
    attend(1, 2)
    mlp(0, 1)
    mlp(0, 2)
    attend(1, 3)
    pass_right(0, 1)
    pass_left(0, 2)
    out_proj(1)
    mlp(1, 0)
    mlp(0, 3)
    pass_right(0, 3)
    pass_left(0, 0)
    pass_right(0, 0)
    pass_left(0, 3)
    pass_right(0, 2)
    pass_left(0, 1)
    ag_forward(*ag_two(1))
    mlp(1, 1)
    mlp(1, 2)
    pass_right(1, 1)
    pass_left(1, 2)
    for pos in (1, 2, 0, 3):
        finish(0, pos)
    mlp(1, 3)
    pass_right(1, 3)
    pass_left(1, 0)
    pass_right(1, 0)
    pass_left(1, 3)
    pass_right(1, 2)
    pass_left(1, 1)
    for pos in (1, 2, 0, 3):
        finish(1, pos)

    for s in sends:
        s.wait_send()
    for q in range(2):
        for pos, r in enumerate(order):
            block = qs.at[q, r, pl.ds(0, 240)]
            rc(block, block, a_s.at[q, r], a_r.at[q, r], right).wait_send()
            block = att_s.at[q, r, pl.ds(0, 16 if pos else 15)]
            rc(block, block, b_s.at[q, r], b_r.at[q, r], right).wait_send()
    for w in writes:
        w.wait()


def body(temporal, frame_ids, proj_weight, embed_table, qkv_weight, out_weight, gate_up, down_weight, norm_gains):
    c = lax.axis_index("codebook")
    h = lax.axis_index("hidden")
    start_id = embed_table.shape[1] - 1
    own_ids = lax.dynamic_slice_in_dim(frame_ids[:, 0], h * 512, 512, 0)
    own_ids = own_ids.reshape(4, 2, 64).transpose(1, 0, 2).reshape(512)
    earlier = lax.ppermute(own_ids, "codebook", [(i, i + 1) for i in range(15)])
    previous = jnp.where(c == 0, start_id, earlier)
    emb = embed_table[0][previous].reshape(2, 256, 1024)
    vm, dma = pltpu.VMEM, pltpu.SemaphoreType.DMA
    any_spec = pl.BlockSpec(memory_space=pl.ANY)
    result = pl.pallas_call(
        kernel,
        name="depth_layer",
        out_shape=jax.ShapeDtypeStruct((4, 4, 2, 64, 256), F32),
        in_specs=[any_spec] * 7 + [pl.BlockSpec(memory_space=pltpu.VMEM)],
        out_specs=any_spec,
        scratch_shapes=[
            vm((2, 16, 64, 1024), BF16), vm((1024, 1024), BF16), vm((3, 1024, 256), BF16), vm((4, 256, 1024), BF16),
            vm((2, 1024, 1024), BF16), vm((1024, 1024), BF16), vm((2, 256, 1024), BF16),
            vm((2, 256, 1024), BF16), vm((2, 256, 1024), BF16), vm((2, 256, 1024), BF16),
            vm((2, 128, 1024), BF16), vm((2, 128, 1024), BF16), vm((2, 256, 1024), BF16), vm((2, 256, 1024), BF16),
            vm((2, 256, 1024), F32),
            vm((2, 4, 256, 1024), BF16), vm((2, 4, 256, 768), BF16), vm((2, 4, 16, 16, 768), BF16),
            vm((2, 4, 16, 16, 256), BF16), vm((2, 4, 256, 256), BF16), vm((256, 256), F32),
            vm((2, 4, 256, 1024), BF16), vm((2, 4, 256, 1024), BF16),
            vm((2, 4, 256, 256), BF16), vm((2, 4, 256, 256), BF16), vm((2, 4, 256, 256), BF16),
            vm((2, 4, 128, 256), BF16), vm((2, 4, 128, 256), BF16),
            vm((2, 4, 256, 256), BF16), vm((2, 4, 256, 256), BF16),
            vm((2, 4, 4, 64, 256), F32),
            dma((8,)), dma((2, 15)), dma((2, 16)), dma((3,)), dma((4,)), dma((2, 6)), dma((2, 6)),
            dma((2, 6)), dma((2, 6)), dma((2, 6)), dma((2, 6)), dma((2, 4)), dma((2, 4)), dma((2, 4)), dma((2, 4)),
            dma((2, 4, 6)), dma((2, 4, 6)), dma((2, 4)),
        ],
        compiler_params=pltpu.CompilerParams(
            collective_id=0, has_side_effects=True, vmem_limit_bytes=67043328
        ),
    )(
        temporal.reshape(2, 64, 1024), emb, proj_weight, qkv_weight, out_weight, gate_up, down_weight, norm_gains
    )
    return result.reshape(1, 2048, 256)


def solution(mesh):
    placed = (
        P(("frames", "codebook"), "hidden"),
        P("frames", "codebook"),
        P("codebook", "hidden", None),
        P("codebook", None, None),
        P("codebook", None, None, "hidden"),
        P("codebook", "hidden", None),
        P("codebook", None, None, "hidden"),
        P("codebook", "hidden", None),
        P("codebook", None, None),
    )
    return jax.shard_map(
        body,
        mesh=mesh,
        in_specs=placed,
        out_specs=P("codebook", "frames", "hidden"),
        check_vma=False,
    )
```

time: 251 us -> 211 us (0.84)
  Pallas kernels: 236 us -> 195 us
    pallas_call x1, Pallas kernels: 236 us -> 195 us  [body(): pl.pallas_call(kernel, name='depth_layer', out_shape=jax.ShapeDtypeStruct...]
where the time goes in v2:
time: 211 us
  Pallas kernels  195 us (92%)
  local copies, waits for them, and re-layouts  10.1 us (5%)
  starting transfers between devices  4.49 us (2%)
    pallas_call x1, Pallas kernels, body(): pl.pallas_call(kernel, name='depth_layer', out_shape=jax.ShapeDtypeStruct...  195 us
    gather x1, local copies, waits for them, and re-layouts, body(): emb = embed_table[0][previous].reshape(2, 256, 1024)  6.2 us
    ppermute x1, starting transfers between devices, body(): earlier = lax.ppermute(own_ids, 'codebook', [(i, i + 1) for i in range(15)])  4.49 us
  transfers between devices with their start and end apart: 1, of which 1 were waited for; matrix products, arithmetic and copies ran while one was open for 0% of the time, Pallas kernels for 0%

profile of v2, /device:TPU:1, one launch (start us, length us, event | category | flops | bytes accessed | tf_op | source)
XLA Modules:
  0.0 210.8 jit_solution(6577444394101156004)
XLA Ops:
  0.0 0.7 dynamic-slice_reduce_fusion
  0.7 0.1 reshape.18
  0.8 0.1 reshape.19
  0.9 4.5 %collective-permute-start = (s32[512]{0:T(512)S(1)}, s32[512]{0:T(512)S(1)}, u32[]{:S(2)}, u32[]{:S(2)}) collective-permute-start(s32[512]{0:T(512)S(1)} %reshape.19), channel_id=1, source_target_pairs={{0,4},{4,8},{8,12},{12,16},{16,20},{20,24},{24,28},{28,32},{32,36}... | collective-permute-start | bytes 6152 | tf_op jit(solution)/shard_map/ppermute | solution.py:406
  5.4 0.7 collective-permute-done
  6.1 6.2 %gather_fusion = bf16[512,1024]{1,0:T(8,128)(2,1)} fusion(bf16[2049,1024]{1,0:T(8,128)(2,1)} %bitcast.5, s32[1024]{0:T(1024)S(1)} %pad_clamp_fusion), kind=kCustom, calls=%fused_computation | custom fusion | bytes 2099200 | tf_op jit(solution)/shard_map/gather | solution.py:408
  12.3 195.5 %depth_layer.1 = f32[4,4,2,64,256]{4,3,2,1,0:T(8,128)} custom-call(bf16[2,64,1024]{2,1,0:T(8,128)(2,1)} %bitcast.8, bf16[2,256,1024]{2,1,0:T(8,128)(2,1)} %bitcast.7, bf16[1,1024,1024]{2,1,0:T(8,128)(2,1)} %wp_in.1, bf16[1,3,1024,256]{3,2,1,0:T(8,128)(2,1)} %wqkv_in.1, bf16[1,256,1024]{2,1,0:T(8,128)(2,1)} %wo_in.1, bf16[1,2,1024,1024]{3,2,1,0:T(8,128)(2,1)} %wgu_in.1, ...), custom_call_target="tpu_custom_call" | custom-call | tf_op jit(solution)/shard_map/depth_layer/pallas_call | solution.py:411
  207.8 3.0 %copy.12 = f32[1,2048,256]{2,1,0:T(8,128)} copy(f32[1,2048,256]{2,1,0:T(8,128)} %bitcast.6) | data formatting | bytes 4194304
  (3 shorter events, 0.0 us)
Async XLA Ops:
  0.9 5.2 %collective-permute-start = (s32[512]{0:T(512)S(1)}, s32[512]{0:T(512)S(1)}, u32[]{:S(2)}, u32[]{:S(2)}) collective-permute-start(s32[512]{0:T(512)S(1)} %reshape.19), channel_id=1, source_target_pairs={{0,4},{4,8},{8,12},{12,16},{16,20},{20,24},{24,28},{28,32},{32,36}... | collective-permute-start | bytes 6152 | tf_op jit(solution)/shard_map/ppermute | solution.py:406

commit v3 on v2

--- a/solution.py
+++ b/solution.py
@@ -16,11 +16,11 @@
 
 def kernel(
     temporal, emb_in, wp_in, wqkv_in, wo_in, wgu_in, wd_in, gains, out,
-    tbuf, wp, wqkv, wo, wgu, wd, emb,
+    tbuf, wp, wq, wo, wgu, wd, emb,
     ps2, psr, psl, pfl, pfr, prl, prr, x0,
-    n1, qs, qr, att_s, att_r, bias,
+    n1, nq, qs, qr, att_s, att_r, bias,
     n2, act, ds2, dsr, dsl, dfl, dfr, drl, drr, oacc,
-    loc, t_s, t_r, wo_s, wo_r, p_s, p_r, n_s, n_r, m_s, m_r, a_s, a_r, b_s, b_r, d_s, d_r, o_s,
+    loc, t_s, t_r, wo_s, wo_r, p_s, p_r, w_s, w_r, v_s, v_r, x_s, x_r, m_s, m_r, a_s, a_r, b_s, b_r, d_s, d_r, o_s,
 ):
     f = lax.axis_index("frames")
     c = lax.axis_index("codebook")
@@ -48,23 +48,32 @@
     loads = [
         pltpu.make_async_copy(s, d, loc.at[i])
         for i, (s, d) in enumerate((
-            (wp_in.at[0], wp), (wqkv_in.at[0], wqkv), (wgu_in.at[0], wgu), (wd_in.at[0], wd), (emb_in, emb),
+            (wp_in.at[0], wp), (wqkv_in.at[0], wq.at[h]), (wgu_in.at[0], wgu), (wd_in.at[0], wd), (emb_in, emb),
             (wo_in.at[0], wo.at[h]), (temporal.at[0], tbuf.at[0, c]), (temporal.at[1], tbuf.at[1, c]),
         ))
     ]
-    for i in (6, 7, 0, 4, 5, 1, 2, 3):
+    home = k == f
+    worker = f * 8 + y * 4 + x
+    book = c - k + f
+    for i in (6, 7, 0, 4, 5, 2, 3):
         loads[i].start()
+
+    @pl.when(home)
+    def _():
+        loads[1].start()
 
     barrier = pltpu.get_barrier_semaphore()
 
     def greet(n, carry):
         pl.semaphore_signal(
-            barrier, inc=1, device_id=(f, (c + n // 4) % 16, (h + n % 4) % 4), device_id_type=MESH
+            barrier, inc=1, device_id=((f + n // 16) % 2, (c + n % 16) % 16, h), device_id_type=MESH
         )
         return carry
 
-    lax.fori_loop(1, 64, greet, 0)
-    pl.semaphore_wait(barrier, 63)
+    pl.semaphore_signal(barrier, inc=1, device_id=right, device_id_type=MESH)
+    pl.semaphore_signal(barrier, inc=1, device_id=left, device_id_type=MESH)
+    lax.fori_loop(1, 32, greet, 0)
+    pl.semaphore_wait(barrier, 33)
 
     partner = (f, y * 8 + x * 2 + 1 - k, h)
 
@@ -135,7 +144,7 @@
             if extras:
                 x0[q, rows, :] = v
             scale = lax.rsqrt(jnp.mean(v * v, axis=-1, keepdims=True) + 1e-05)
-            dst[q, h, rows, :] = (v * scale * gain).astype(BF16)
+            dst[rows, :] = (v * scale * gain).astype(BF16)
             return carry
 
         lax.fori_loop(0, 8, chunk, 0)
@@ -143,7 +152,23 @@
     def norm_one(q):
         for i, ref in ((2, prl.at[q, bot]), (3, prr.at[q, top]), (4, prl.at[q, top]), (5, prr.at[q, bot])):
             got(ref, p_s.at[q, i], p_r.at[q, i])
-        norm_rows(q, n1, gains[0, 0:1, :], (prl, prr))
+
+        @pl.when(home)
+        def _():
+            norm_rows(q, nq.at[q], gains[0, 0:1, :], (prl, prr))
+
+        @pl.when(jnp.logical_not(home))
+        def _():
+            norm_rows(q, n1.at[q], gains[0, 0:1, :], (prl, prr))
+            swap(q).start()
+
+    def swap(q):
+        return rc(n1.at[q], nq.at[q], x_s.at[q], x_r.at[q], (1 - f, c - k + 1 - k, h))
+
+    def swap_in(q):
+        @pl.when(jnp.logical_not(home))
+        def _():
+            swap(q).wait_recv()
 
     def ag_start(buf, ss, rs):
         send(buf.at[h, top], buf.at[h, top], ss.at[0], rs.at[0], right)
@@ -166,28 +191,71 @@
             got(buf.at[ho, top], ss.at[4], rs.at[4])
             got(buf.at[ho, bot], ss.at[5], rs.at[5])
 
-    ag_one = lambda q: (n1.at[q], n_s.at[q], n_r.at[q])
     ag_two = lambda q: (n2.at[q], m_s.at[q], m_r.at[q])
 
-    def peer(d):
-        return ((y + d // 8) % 2) * 8 + ((x + (d // 2) % 4) % 4) * 2 + (k + d) % 2
+    upper, lower = pl.ds(0, 512), pl.ds(512, 512)
+
+    def w_copy(i):
+        part = lambda r, rows: wq.at[r, :, rows]
+        block, dev = (
+            (part(h, upper), right), (part(h, lower), right), (part(h, lower), left), (part(h, upper), left),
+            (part(hl, upper), right), (part(hr, lower), left),
+        )[i]
+        return rc(block, block, w_s.at[i], w_r.at[i], dev)
+
+    def w_share(pos):
+        block = wq.at[order[pos]]
+        return rc(block, block, v_s.at[pos], v_r.at[pos], partner)
+
+    def w_start():
+        @pl.when(home)
+        def _():
+            loads[1].wait()
+            for i in (0, 2, 1, 3):
+                w_copy(i).start()
+            w_share(0).start()
+
+    def w_forward():
+        @pl.when(home)
+        def _():
+            got(wq.at[hl, :, upper], w_s.at[0], w_r.at[0])
+            w_copy(4).start()
+            got(wq.at[hr, :, lower], w_s.at[2], w_r.at[2])
+            w_copy(5).start()
+
+    def w_in(pos):
+        @pl.when(home)
+        def _():
+            if pos == 1:
+                got(wq.at[hl, :, lower], w_s.at[1], w_r.at[1])
+            if pos == 2:
+                got(wq.at[hr, :, upper], w_s.at[3], w_r.at[3])
+            if pos == 3:
+                got(wq.at[ho, :, upper], w_s.at[4], w_r.at[4])
+                got(wq.at[ho, :, lower], w_s.at[5], w_r.at[5])
+            if pos:
+                w_share(pos).start()
+
+        @pl.when(jnp.logical_not(home))
+        def _():
+            w_share(pos).wait_recv()
 
     def qkv(q, pos):
         r = order[pos]
-        ag_wait(*ag_one(q), pos)
         for i in range(3):
-            part = jnp.dot(n1[q, r], wqkv[i], preferred_element_type=F32)
+            part = jnp.dot(nq[q], wq[r, i], preferred_element_type=F32)
             qs[q, r, :, i * 256:(i + 1) * 256] = part.astype(BF16)
 
         def post(d, carry):
-            dst = peer(d)
+            df, dy, dx = (f + d // 8) % 2, (y + (d // 4) % 2) % 2, (x + d % 4) % 4
             rc(
-                qs.at[q, r, pl.ds(dst * 16, 16)], qr.at[q, r, c], a_s.at[q, r], a_r.at[q, r], (f, dst, h)
+                qs.at[q, r, pl.ds((df * 8 + dy * 4 + dx) * 16, 16)], qr.at[q, r, book],
+                a_s.at[q, r], a_r.at[q, r], (df, dy * 8 + dx * 2 + k, h),
             ).start()
             return carry
 
         lax.fori_loop(1, 16, post, 0)
-        qr[q, r, c] = qs[q, r, pl.ds(pl.multiple_of(c * 16, 16), 16), :]
+        qr[q, r, book] = qs[q, r, pl.ds(pl.multiple_of(worker * 16, 16), 16), :]
 
     def attend(q, pos):
         r = order[pos]
@@ -221,20 +289,35 @@
 
         lax.fori_loop(0, 2, unit, 0)
 
+        def back(d):
+            to = (c + d) % 16
+            return rc(
+                att_s.at[q, r, to], att_r.at[q, r, pl.ds(worker * 16, 16)], b_s.at[q, r], b_r.at[q, r], (k, to, h)
+            )
+
         def post(d, carry):
-            dst = peer(d)
-            rc(
-                att_s.at[q, r, dst], att_r.at[q, h, pl.ds(c * 16, 16)], b_s.at[q, r], b_r.at[q, h], (f, dst, r)
-            ).start()
-            return carry
-
-        lax.fori_loop(0 if pos else 1, 16, post, 0)
-        if pos == 0:
-            att_r[q, h, pl.ds(pl.multiple_of(c * 16, 16), 16), :] = att_s[q, h, c]
+            back(d).start()
+            return carry
+
+        lax.fori_loop(1, 16, post, 0)
+
+        @pl.when(home)
+        def _():
+            att_r[q, r, pl.ds(pl.multiple_of(worker * 16, 16), 16), :] = att_s[q, r, c]
+
+        @pl.when(jnp.logical_not(home))
+        def _():
+            back(0).start()
 
     def out_proj(q):
-        for pos, src in enumerate(order):
-            got(att_r.at[q, src, pl.ds(0, 256 if pos else 240)], b_s.at[q, src], b_r.at[q, src])
+        for src in order:
+            @pl.when(home)
+            def _():
+                got(att_r.at[q, src, pl.ds(0, 240)], b_s.at[q, src], b_r.at[q, src])
+
+            @pl.when(jnp.logical_not(home))
+            def _():
+                got(att_r.at[q, src], b_s.at[q, src], b_r.at[q, src])
 
         def tile(n, carry):
             cols = pl.ds(pl.multiple_of(n * 256, 256), 256)
@@ -245,7 +328,7 @@
             return carry
 
         lax.fori_loop(0, 4, tile, 0)
-        norm_rows(q, n2, gains[0, 1:2, :], ())
+        norm_rows(q, n2.at[q, h], gains[0, 1:2, :], ())
         ag_start(*ag_two(q))
 
     def mine(q, pos, row0, rows, target):
@@ -306,10 +389,8 @@
         writes.append(w)
 
     temporal_out(0)
+    w_start()
     temporal_out(1)
-    loads[5].wait()
-    for j in (1, 3, 2):
-        send(wo.at[h], wo.at[h], wo_s.at[j - 1], wo_r.at[h], (f, c, (h + j) % 4))
     row = lax.broadcasted_iota(jnp.int32, (256, 256), 0)
     col = lax.broadcasted_iota(jnp.int32, (256, 256), 1)
     bias[...] = jnp.where((row % 16 == col % 16) & (row // 16 >= col // 16), 0.0, -1e30)
@@ -320,48 +401,54 @@
     loads[4].wait()
     proj_own(0)
     proj_pass(0)
+    w_forward()
     temporal_in(1)
     proj_far(1)
     norm_one(0)
-    ag_start(*ag_one(0))
-    loads[1].wait()
+    proj_near(1)
+    w_in(0)
+    swap_in(0)
     qkv(0, 0)
-    proj_near(1)
+    w_in(1)
+    qkv(0, 1)
+    w_in(2)
+    qkv(0, 2)
+    w_in(3)
+    qkv(0, 3)
     proj_own(1)
-    ag_forward(*ag_one(0))
     proj_pass(1)
+    loads[5].wait()
+    ag_wo = (wo, wo_s, wo_r)
+    ag_start(*ag_wo)
     attend(0, 0)
-    qkv(0, 1)
-    qkv(0, 2)
-    qkv(0, 3)
     attend(0, 1)
+    norm_one(1)
+    ag_forward(*ag_wo)
     attend(0, 2)
-    norm_one(1)
-    ag_start(*ag_one(1))
+    attend(0, 3)
+    swap_in(1)
     qkv(1, 0)
-    attend(0, 3)
-    for src in order[1:]:
-        got(wo.at[src], wo_s.at[0], wo_r.at[src])
+    qkv(1, 1)
+    for pos in (1, 2, 3):
+        ag_wait(*ag_wo, pos)
     out_proj(0)
-    ag_forward(*ag_one(1))
+    qkv(1, 2)
+    qkv(1, 3)
     loads[2].wait()
     loads[3].wait()
     mlp(0, 0)
     attend(1, 0)
-    qkv(1, 1)
-    qkv(1, 2)
     ag_forward(*ag_two(0))
-    qkv(1, 3)
     attend(1, 1)
     attend(1, 2)
     mlp(0, 1)
+    attend(1, 3)
     mlp(0, 2)
-    attend(1, 3)
     pass_right(0, 1)
     pass_left(0, 2)
+    mlp(0, 3)
     out_proj(1)
     mlp(1, 0)
-    mlp(0, 3)
     pass_right(0, 3)
     pass_left(0, 0)
     pass_right(0, 0)
@@ -388,11 +475,29 @@
     for s in sends:
         s.wait_send()
     for q in range(2):
-        for pos, r in enumerate(order):
+        for r in range(4):
             block = qs.at[q, r, pl.ds(0, 240)]
             rc(block, block, a_s.at[q, r], a_r.at[q, r], right).wait_send()
-            block = att_s.at[q, r, pl.ds(0, 16 if pos else 15)]
-            rc(block, block, b_s.at[q, r], b_r.at[q, r], right).wait_send()
+
+    @pl.when(home)
+    def _():
+        for i in range(6):
+            w_copy(i).wait_send()
+        for pos in range(4):
+            w_share(pos).wait_send()
+        for q in range(2):
+            for r in range(4):
+                block = att_s.at[q, r, pl.ds(0, 15)]
+                rc(block, block, b_s.at[q, r], b_r.at[q, r], right).wait_send()
+
+    @pl.when(jnp.logical_not(home))
+    def _():
+        for q in range(2):
+            swap(q).wait_send()
+            for r in range(4):
+                block = att_s.at[q, r]
+                rc(block, block, b_s.at[q, r], b_r.at[q, r], right).wait_send()
+
     for w in writes:
         w.wait()
 
@@ -415,20 +520,20 @@
         in_specs=[any_spec] * 7 + [pl.BlockSpec(memory_space=pltpu.VMEM)],
         out_specs=any_spec,
         scratch_shapes=[
-            vm((2, 16, 64, 1024), BF16), vm((1024, 1024), BF16), vm((3, 1024, 256), BF16), vm((4, 256, 1024), BF16),
+            vm((2, 16, 64, 1024), BF16), vm((1024, 1024), BF16), vm((4, 3, 1024, 256), BF16), vm((4, 256, 1024), BF16),
             vm((2, 1024, 1024), BF16), vm((1024, 1024), BF16), vm((2, 256, 1024), BF16),
             vm((2, 256, 1024), BF16), vm((2, 256, 1024), BF16), vm((2, 256, 1024), BF16),
             vm((2, 128, 1024), BF16), vm((2, 128, 1024), BF16), vm((2, 256, 1024), BF16), vm((2, 256, 1024), BF16),
             vm((2, 256, 1024), F32),
-            vm((2, 4, 256, 1024), BF16), vm((2, 4, 256, 768), BF16), vm((2, 4, 16, 16, 768), BF16),
+            vm((2, 256, 1024), BF16), vm((2, 256, 1024), BF16), vm((2, 4, 256, 768), BF16), vm((2, 4, 16, 16, 768), BF16),
             vm((2, 4, 16, 16, 256), BF16), vm((2, 4, 256, 256), BF16), vm((256, 256), F32),
             vm((2, 4, 256, 1024), BF16), vm((2, 4, 256, 1024), BF16),
             vm((2, 4, 256, 256), BF16), vm((2, 4, 256, 256), BF16), vm((2, 4, 256, 256), BF16),
             vm((2, 4, 128, 256), BF16), vm((2, 4, 128, 256), BF16),
             vm((2, 4, 256, 256), BF16), vm((2, 4, 256, 256), BF16),
             vm((2, 4, 4, 64, 256), F32),
-            dma((8,)), dma((2, 15)), dma((2, 16)), dma((3,)), dma((4,)), dma((2, 6)), dma((2, 6)),
-            dma((2, 6)), dma((2, 6)), dma((2, 6)), dma((2, 6)), dma((2, 4)), dma((2, 4)), dma((2, 4)), dma((2, 4)),
+            dma((8,)), dma((2, 15)), dma((2, 16)), dma((6,)), dma((6,)), dma((2, 6)), dma((2, 6)),
+            dma((6,)), dma((6,)), dma((4,)), dma((4,)), dma((2,)), dma((2,)), dma((2, 6)), dma((2, 6)), dma((2, 4)), dma((2, 4)), dma((2, 4)), dma((2, 4)),
             dma((2, 4, 6)), dma((2, 4, 6)), dma((2, 4)),
         ],
         compiler_params=pltpu.CompilerParams(

time: 211 us -> 190 us (0.900)
  Pallas kernels: 195 us -> 174 us
    pallas_call x1, Pallas kernels: 195 us -> 174 us  [body(): pl.pallas_call(kernel, name='depth_layer', out_shape=jax.ShapeDtypeStruct...]
where the time goes in v3:
time: 190 us; the launch traced here: 189 us
  Pallas kernels  174 us (92%)
  local copies, waits for them, and re-layouts  10.1 us (5%)
  starting transfers between devices  4.49 us (2%)
    pallas_call x1, Pallas kernels, body(): pl.pallas_call(kernel, name='depth_layer', out_shape=jax.ShapeDtypeStruct...  174 us
    gather x1, local copies, waits for them, and re-layouts, body(): emb = embed_table[0][previous].reshape(2, 256, 1024)  6.2 us
    ppermute x1, starting transfers between devices, body(): earlier = lax.ppermute(own_ids, 'codebook', [(i, i + 1) for i in range(15)])  4.49 us
  transfers between devices with their start and end apart: 1, of which 1 were waited for; matrix products, arithmetic and copies ran while one was open for 0% of the time, Pallas kernels for 0%

profile of v3, /device:TPU:1, one launch (start us, length us, event | category | flops | bytes accessed | tf_op | source)
XLA Modules:
  0.0 189.4 jit_solution(4054432984991782157)
XLA Ops:
  0.0 0.7 dynamic-slice_reduce_fusion
  0.7 0.1 reshape.18
  0.8 0.1 reshape.19
  0.9 4.5 %collective-permute-start = (s32[512]{0:T(512)S(1)}, s32[512]{0:T(512)S(1)}, u32[]{:S(2)}, u32[]{:S(2)}) collective-permute-start(s32[512]{0:T(512)S(1)} %reshape.19), channel_id=1, source_target_pairs={{0,4},{4,8},{8,12},{12,16},{16,20},{20,24},{24,28},{28,32},{32,36}... | collective-permute-start | bytes 6152 | tf_op jit(solution)/shard_map/ppermute | solution.py:511
  5.4 0.7 collective-permute-done
  6.1 6.2 %gather_fusion = bf16[512,1024]{1,0:T(8,128)(2,1)} fusion(bf16[2049,1024]{1,0:T(8,128)(2,1)} %bitcast.5, s32[1024]{0:T(1024)S(1)} %pad_clamp_fusion), kind=kCustom, calls=%fused_computation | custom fusion | bytes 2099200 | tf_op jit(solution)/shard_map/gather | solution.py:513
  12.3 174.0 %depth_layer.1 = f32[4,4,2,64,256]{4,3,2,1,0:T(8,128)} custom-call(bf16[2,64,1024]{2,1,0:T(8,128)(2,1)} %bitcast.8, bf16[2,256,1024]{2,1,0:T(8,128)(2,1)} %bitcast.7, bf16[1,1024,1024]{2,1,0:T(8,128)(2,1)} %wp_in.1, bf16[1,3,1024,256]{3,2,1,0:T(8,128)(2,1)} %wqkv_in.1, bf16[1,256,1024]{2,1,0:T(8,128)(2,1)} %wo_in.1, bf16[1,2,1024,1024]{3,2,1,0:T(8,128)(2,1)} %wgu_in.1, ...), custom_call_target="tpu_custom_call" | custom-call | tf_op jit(solution)/shard_map/depth_layer/pallas_call | solution.py:516
  186.3 3.0 %copy.12 = f32[1,2048,256]{2,1,0:T(8,128)} copy(f32[1,2048,256]{2,1,0:T(8,128)} %bitcast.6) | data formatting | bytes 4194304
  (3 shorter events, 0.0 us)
Async XLA Ops:
  0.9 5.2 %collective-permute-start = (s32[512]{0:T(512)S(1)}, s32[512]{0:T(512)S(1)}, u32[]{:S(2)}, u32[]{:S(2)}) collective-permute-start(s32[512]{0:T(512)S(1)} %reshape.19), channel_id=1, source_target_pairs={{0,4},{4,8},{8,12},{12,16},{16,20},{20,24},{24,28},{28,32},{32,36}... | collective-permute-start | bytes 6152 | tf_op jit(solution)/shard_map/ppermute | solution.py:511

commit v4 on v2

v4 whole, which is shorter than its diff:
```python
import functools

import jax
import jax.numpy as jnp
from jax import lax
from jax.experimental import pallas as pl
from jax.experimental.pallas import tpu as pltpu
from jax.sharding import PartitionSpec as P

HEADS = 16
MESH = pl.DeviceIdType.MESH
F32 = jnp.float32
BF16 = jnp.bfloat16
PLANE = (
    (1, 0, 2), (0, 1, 2), (1, 0, 1), (1, 0, 3), (1, 1, 2), (0, 0, 2), (0, 1, 1), (0, 1, 3),
    (1, 0, 0), (1, 1, 1), (1, 1, 3), (0, 0, 1), (0, 0, 3), (0, 1, 0), (1, 1, 0),
)
ROW = (1, 3, 2)


def kernel(
    temporal, ids_in, table_in, wp_in, wqkv_in, wo_in, wgu_in, wd_in, gains, out,
    tbuf, wp, wq, wo, wgu, wd, emb, first, ids_own, ids, spread, hot,
    ps2, psr, psl, pfl, pfr, prl, prr, x0,
    own_s, own_r, nq, qs, qr, att_s, att_r, bias, gain,
    n2, act, ds2, dsr, dsl, dfl, dfr, drl, drr, dos, dor, oacc,
    loc, i_s, i_r, t_s, t_r, wo_s, wo_r, p_s, p_r, w_s, w_r, v_s, v_r, u_s, u_r, g_s, g_r, e_s, e_r, x_s, x_r, m_s, m_r, a_s, a_r, b_s, b_r, d_s, d_r, o_s, gate,
):
    f = lax.axis_index("frames")
    c = lax.axis_index("codebook")
    h = lax.axis_index("hidden")
    hr, hl, ho = (h + 1) % 4, (h + 3) % 4, (h + 2) % 4
    right, left = (f, c, hr), (f, c, hl)
    y, x, k = c // 8, (c // 2) % 4, c % 2
    order = (h, hl, hr, ho)
    top, bot = pl.ds(0, 128), pl.ds(128, 128)
    sends = []

    def rc(src, dst, ss, rs, dev):
        return pltpu.make_async_remote_copy(
            src_ref=src, dst_ref=dst, send_sem=ss, recv_sem=rs, device_id=dev, device_id_type=MESH
        )

    def send(src, dst, ss, rs, dev):
        s = rc(src, dst, ss, rs, dev)
        s.start()
        sends.append(s)

    def got(ref, ss, rs):
        rc(ref, ref, ss, rs, right).wait_recv()

    loads = [
        pltpu.make_async_copy(s, d, loc.at[i])
        for i, (s, d) in enumerate((
            (wp_in.at[0], wp), (wqkv_in.at[0], wq.at[h]), (wgu_in.at[0], wgu), (wd_in.at[0], wd), (ids_in.at[h], ids_own),
            (wo_in.at[0], wo.at[h]), (temporal.at[0], tbuf.at[0, c]), (temporal.at[1], tbuf.at[1, c]),
            (table_in.at[0, pl.ds(0, 2048)], act), (table_in.at[0, pl.ds(2048, 1)], first),
        ))
    ]
    home = k == f
    away = jnp.logical_not(home)
    worker = f * 8 + y * 4 + x
    book = c - k + f
    partner = (f, c + 1 - 2 * k, h)
    owner = lambda at: (k, book, at)
    for i in (4, 6, 7, 0):
        loads[i].start()

    @pl.when(home)
    def _():
        for i in (1, 9, 8, 5, 2, 3):
            loads[i].start()

    barrier = pltpu.get_barrier_semaphore()

    def greet(n, carry):
        pl.semaphore_signal(
            barrier, inc=1, device_id=((f + n // 16) % 2, (c + n % 16) % 16, h), device_id_type=MESH
        )
        return carry

    pl.semaphore_signal(barrier, inc=1, device_id=right, device_id_type=MESH)
    pl.semaphore_signal(barrier, inc=1, device_id=left, device_id_type=MESH)
    for at in (hr, hl):
        pl.semaphore_signal(barrier, inc=1, device_id=(1 - f, c + 1 - 2 * k, at), device_id_type=MESH)
    lax.fori_loop(1, 32, greet, 0)
    pl.semaphore_wait(barrier, 35)

    common = (
        (table_in.at[0, pl.ds(2048, 1)], first, 9), (table_in.at[0, pl.ds(0, 2048)], act, 8),
        (gains.at[0], gain, None), (wgu_in.at[0], wgu, 2), (wd_in.at[0], wd, 3),
    )

    def share(i):
        return rc(common[i][0], common[i][1], g_s.at[i], g_r.at[i], partner)

    def share_out():
        @pl.when(home)
        def _():
            gain[...] = gains[0]
            for i in range(5):
                share(i).start()

    def ready(i):
        @pl.when(home)
        def _():
            if common[i][2] is not None:
                loads[common[i][2]].wait()

        @pl.when(away)
        def _():
            share(i).wait_recv()

    def ids_out():
        loads[4].wait()
        send(ids_own, ids, i_s.at[0], i_r.at[0], ((c + 1) % 2, ((c + 1) % 16) // 2 * 2 + f, h))

    def ids_spread():
        got(ids, i_s.at[0], i_r.at[0])
        for s in range(4):
            turned = jnp.transpose(jnp.broadcast_to(ids[s:s + 1, :].astype(F32), (128, 128))).astype(jnp.int32)
            for q in range(2):
                spread[q, s * 64:s * 64 + 64, :] = turned[q * 64:q * 64 + 64]

    def embed(q):
        @pl.when(book == 0)
        def _():
            emb[q] = jnp.broadcast_to(first[...], (256, 1024))

        @pl.when(book != 0)
        def _():
            lane = lax.broadcasted_iota(jnp.int32, (256, 128), 1)
            for b in range(16):
                hot[:, b * 128:(b + 1) * 128] = jnp.where(spread[q] == lane + b * 128, 1.0, 0.0).astype(BF16)

            def tile(n, carry):
                cols = pl.ds(pl.multiple_of(n * 256, 256), 256)
                emb[q, :, cols] = jnp.dot(hot[...], act[:, cols], preferred_element_type=F32).astype(BF16)
                return carry

            lax.fori_loop(0, 4, tile, 0)

    def core_of(oy, ox, core):
        return ((y + oy) % 2) * 8 + ((x + ox) % 4) * 2 + core

    def temporal_move(q, src, i, dev):
        send(tbuf.at[q, src], tbuf.at[q, src], t_s.at[q, i], t_r.at[q, src], dev)

    def temporal_out(q):
        loads[6 + q].wait()
        temporal_move(q, c, 0, (f, core_of(1, 0, k), h))
        for i, ox in enumerate(ROW):
            temporal_move(q, c, 1 + i, (f, core_of(0, ox, k), h))
        temporal_move(q, c, 4, partner)

    def temporal_pass(q):
        across = core_of(1, 0, k)
        got(tbuf.at[q, across], t_s.at[q, 0], t_r.at[q, across])
        for i, ox in enumerate(ROW):
            temporal_move(q, across, 5 + i, (f, core_of(0, ox, k), h))
        temporal_move(q, across, 8, partner)

    def temporal_in(q):
        for oy in range(2):
            for i, ox in enumerate(ROW):
                src = core_of(oy, 4 - ox, k)
                got(tbuf.at[q, src], t_s.at[q, 0], t_r.at[q, src])
                temporal_move(q, src, 9 + oy * 3 + i, partner)
        for oy in range(2):
            for ox in range(4):
                src = core_of(oy, ox, 1 - k)
                got(tbuf.at[q, src], t_s.at[q, 0], t_r.at[q, src])

    def proj(q, block, row0, rows, store):
        def tile(n, carry):
            cols = pl.ds(pl.multiple_of(n * 256, 256), 256)
            lhs = tbuf[q, pl.ds(block * 4 + row0 // 64, rows // 64)].reshape(rows, 1024)
            store(cols, jnp.dot(lhs, wp[:, cols], preferred_element_type=F32))
            return carry

        lax.fori_loop(0, 4, tile, 0)

    def into(ref, row0, rows, extra=None):
        def store(cols, value):
            if extra is not None:
                value = value + extra[:, cols].astype(F32)
            ref[pl.ds(row0, rows), cols] = value.astype(ref.dtype)

        return store

    def proj_far(q):
        ss, rs = p_s.at[q], p_r.at[q]
        proj(q, ho, 0, 256, into(ps2.at[q], 0, 256))
        send(ps2.at[q, top], pfl.at[q], ss.at[0], rs.at[0], right)
        send(ps2.at[q, bot], pfr.at[q], ss.at[1], rs.at[1], left)

    def proj_near(q):
        ss, rs = p_s.at[q], p_r.at[q]
        proj(q, hr, 128, 128, into(psr.at[q], 128, 128))
        send(psr.at[q, bot], prl.at[q, bot], ss.at[2], rs.at[2], right)
        proj(q, hl, 0, 128, into(psl.at[q], 0, 128))
        send(psl.at[q, top], prr.at[q, top], ss.at[3], rs.at[3], left)

    def own_copy(q):
        return rc(own_s.at[q], own_r.at[q], x_s.at[q], x_r.at[q], owner(h))

    def proj_own(q):
        proj(q, h, 0, 256, into(x0.at[q], 0, 256))

    def near_in(q):
        got(prl.at[q, bot], p_s.at[q, 2], p_r.at[q, 2])
        got(prr.at[q, top], p_s.at[q, 3], p_r.at[q, 3])

    def own_send(q):
        @pl.when(away)
        def _():
            near_in(q)
            for half, near in ((top, prr), (bot, prl)):
                own_s[q, half, :] = (x0[q, half, :] + near[q, half, :].astype(F32)).astype(BF16)
            own_copy(q).start()

    def proj_pass(q):
        ss, rs = p_s.at[q], p_r.at[q]
        got(pfl.at[q], ss.at[0], rs.at[0])
        proj(q, hr, 0, 128, into(psr.at[q], 0, 128, pfl.at[q]))
        send(psr.at[q, top], prl.at[q, top], ss.at[4], rs.at[4], owner(hr))
        got(pfr.at[q], ss.at[1], rs.at[1])
        proj(q, hl, 128, 128, into(psl.at[q], 128, 128, pfr.at[q]))
        send(psl.at[q, bot], prr.at[q, bot], ss.at[5], rs.at[5], owner(hl))

    def norm_rows(q, dst, scale_by, base, extras, first_row=0, last_row=256):
        def chunk(n, carry):
            rows = pl.ds(pl.multiple_of(first_row + n * 32, 32), 32)
            v = base[q, rows, :].astype(F32)
            for e in extras:
                v = v + e[q, rows, :].astype(F32)
            if extras:
                x0[q, rows, :] = v
            scale = lax.rsqrt(jnp.mean(v * v, axis=-1, keepdims=True) + 1e-05)
            dst[rows, :] = (v * scale * scale_by).astype(BF16)
            return carry

        lax.fori_loop(0, (last_row - first_row) // 32, chunk, 0)

    def norm_one(q):
        got(prl.at[q, top], p_s.at[q, 4], p_r.at[q, 4])
        got(prr.at[q, bot], p_s.at[q, 5], p_r.at[q, 5])

        @pl.when(home)
        def _():
            near_in(q)
            norm_rows(q, nq.at[q], gain[0:1, :], x0, (prl, prr, emb))

        @pl.when(away)
        def _():
            own_copy(q).wait_recv()
            norm_rows(q, nq.at[q], gain[0:1, :], own_r, (prl, emb), 0, 128)
            norm_rows(q, nq.at[q], gain[0:1, :], own_r, (prr, emb), 128, 256)

    def together(q):
        @pl.when(away)
        def _():
            pl.semaphore_signal(gate.at[q], inc=1, device_id=partner, device_id_type=MESH)

        @pl.when(home)
        def _():
            pl.semaphore_wait(gate.at[q], 1)

    def ag_start(buf, ss, rs):
        send(buf.at[h, top], buf.at[h, top], ss.at[0], rs.at[0], right)
        send(buf.at[h, bot], buf.at[h, bot], ss.at[2], rs.at[2], left)
        send(buf.at[h, bot], buf.at[h, bot], ss.at[1], rs.at[1], right)
        send(buf.at[h, top], buf.at[h, top], ss.at[3], rs.at[3], left)

    def ag_forward(buf, ss, rs):
        got(buf.at[hl, top], ss.at[0], rs.at[0])
        send(buf.at[hl, top], buf.at[hl, top], ss.at[4], rs.at[4], right)
        got(buf.at[hr, bot], ss.at[2], rs.at[2])
        send(buf.at[hr, bot], buf.at[hr, bot], ss.at[5], rs.at[5], left)

    def ag_wait(buf, ss, rs, pos):
        if pos == 1:
            got(buf.at[hl, bot], ss.at[1], rs.at[1])
        if pos == 2:
            got(buf.at[hr, top], ss.at[3], rs.at[3])
        if pos == 3:
            got(buf.at[ho, top], ss.at[4], rs.at[4])
            got(buf.at[ho, bot], ss.at[5], rs.at[5])

    ag_two = lambda q: (n2.at[q], m_s.at[q], m_r.at[q])

    class Gathered:
        def __init__(self, part, halves, load, ss, rs, vs, vr):
            self.part, self.halves, self.load = part, halves, load
            self.sems = (ss, rs, vs, vr)

        def copy(self, i):
            low, high = self.halves
            at, rows, dev = ((h, low, right), (h, high, right), (h, high, left), (h, low, left),
                             (hl, low, right), (hr, high, left))[i]
            block = self.part(at, rows)
            return rc(block, block, self.sems[0].at[i], self.sems[1].at[i], dev)

        def arrive(self, i):
            low, high = self.halves
            at, rows = ((hl, low), (hl, high), (hr, high), (hr, low), (ho, low), (ho, high))[i]
            got(self.part(at, rows), self.sems[0].at[i], self.sems[1].at[i])

        def give(self, pos):
            block = self.part(order[pos], None)
            return rc(block, block, self.sems[2].at[pos], self.sems[3].at[pos], partner)

        def start(self):
            @pl.when(home)
            def _():
                loads[self.load].wait()
                for i in (0, 2, 1, 3):
                    self.copy(i).start()
                self.give(0).start()

        def forward(self):
            @pl.when(home)
            def _():
                self.arrive(0)
                self.copy(4).start()
                self.arrive(2)
                self.copy(5).start()

        def take(self, pos):
            @pl.when(home)
            def _():
                for i in ((), (1,), (3,), (4, 5))[pos]:
                    self.arrive(i)
                if pos:
                    self.give(pos).start()

            @pl.when(away)
            def _():
                self.give(pos).wait_recv()

        def drain(self):
            for i in range(6):
                self.copy(i).wait_send()
            for pos in range(4):
                self.give(pos).wait_send()

    w_qkv = Gathered(
        lambda at, rows: wq.at[at] if rows is None else wq.at[at, :, rows],
        (pl.ds(0, 512), pl.ds(512, 512)), 1, w_s, w_r, v_s, v_r,
    )
    w_out = Gathered(
        lambda at, rows: wo.at[at] if rows is None else wo.at[at, rows], (top, bot), 5, wo_s, wo_r, u_s, u_r
    )

    def qkv(q, pos):
        r = order[pos]
        for i in range(3):
            part = jnp.dot(nq[q], wq[r, i], preferred_element_type=F32)
            qs[q, r, :, i * 256:(i + 1) * 256] = part.astype(BF16)

        for of, oy, ox in PLANE:
            df, dy, dx = (f + of) % 2, (y + oy) % 2, (x + ox) % 4
            rc(
                qs.at[q, r, pl.ds((df * 8 + dy * 4 + dx) * 16, 16)], qr.at[q, r, book],
                a_s.at[q, r], a_r.at[q, r], (df, dy * 8 + dx * 2 + k, h),
            ).start()
        qr[q, r, book] = qs[q, r, pl.ds(pl.multiple_of(worker * 16, 16), 16), :]

    def attend(q, pos):
        r = order[pos]
        got(qr.at[q, r, pl.ds(0, 15)], a_s.at[q, r], a_r.at[q, r])

        def unit(n, carry):
            pair = n * 128
            take = lambda i: qr[
                q, r, :, :, pl.ds(pl.multiple_of(i * 256 + pair, 128), 128)
            ].reshape(256, 128)
            qq, kk, v = take(0), take(1), take(2)
            lane = lax.broadcasted_iota(jnp.int32, (256, 128), 1)
            halves = []
            for half in range(2):
                mine = (lane // 64) == half
                qh = jnp.where(mine, qq, jnp.zeros_like(qq))
                parts = []
                for rows, width in ((slice(0, 128), 128), (slice(128, 256), 256)):
                    s = lax.dot_general(
                        qh[rows], kk[:width], (((1,), (1,)), ((), ())), preferred_element_type=F32
                    )
                    s = s * 0.125 + bias[rows, :width]
                    e = jnp.exp(s - jnp.max(s, axis=-1, keepdims=True))
                    total = jnp.sum(e, axis=-1, keepdims=True)
                    o = jnp.dot(e.astype(BF16), v[:width], preferred_element_type=F32)
                    parts.append(o / total)
                halves.append(jnp.concatenate(parts, axis=0))
            o = jnp.where((lane // 64) == 0, halves[0], halves[1]).astype(BF16)
            att_s[q, r, :, :, pl.ds(pl.multiple_of(pair, 128), 128)] = o.reshape(16, 16, 128)
            return carry

        lax.fori_loop(0, 2, unit, 0)

        for of, oy, ox in PLANE:
            df, dy, dx = (f + of) % 2, (y + oy) % 2, (x + ox) % 4
            rc(
                att_s.at[q, r, dy * 8 + dx * 2 + df], att_r.at[q, r, pl.ds(worker * 16, 16)],
                b_s.at[q, r], b_r.at[q, r], (df, dy * 8 + dx * 2 + k, h),
            ).start()
        att_r[q, r, pl.ds(pl.multiple_of(worker * 16, 16), 16), :] = att_s[q, r, book]

    def out_proj(q):
        for src in order:
            got(att_r.at[q, src, pl.ds(0, 240)], b_s.at[q, src], b_r.at[q, src])

        def tile(n, carry):
            cols = pl.ds(pl.multiple_of(n * 256, 256), 256)
            total = x0[q, :, cols]
            for src in range(4):
                total = total + jnp.dot(att_r[q, src], wo[src, :, cols], preferred_element_type=F32)
            x0[q, :, cols] = total
            return carry

        lax.fori_loop(0, 4, tile, 0)
        norm_rows(q, n2.at[q, h], gain[1:2, :], x0, ())
        ag_start(*ag_two(q))

    def mine(q, pos, row0, rows, target):
        cols = pl.ds(pl.multiple_of(target * 256, 256), 256)
        value = jnp.dot(act[pl.ds((q * 4 + pos) * 256 + row0, rows), :], wd[:, cols], preferred_element_type=F32)
        if pos == 0:
            value = value + x0[q, pl.ds(row0, rows), cols]
        return value

    to_right = lambda q: owner(hr) if q else right
    to_left = lambda q: owner(hl) if q else left

    def last_copy(q, pos):
        r = order[pos]
        return rc(dos.at[q, pos], dor.at[q, r], e_s.at[q, pos], e_r.at[q, r], owner(h))

    def mlp(q, pos):
        r = order[pos]
        ss, rs = d_s.at[q, pos], d_r.at[q, r]
        ag_wait(*ag_two(q), pos)

        def tile(n, carry):
            cols = pl.ds(pl.multiple_of(n * 256, 256), 256)
            g = jnp.dot(n2[q, r], wgu[0, :, cols], preferred_element_type=F32)
            u = jnp.dot(n2[q, r], wgu[1, :, cols], preferred_element_type=F32)
            act[pl.ds((q * 4 + pos) * 256, 256), cols] = (g / (1.0 + jnp.exp(-g)) * u).astype(BF16)
            return carry

        lax.fori_loop(0, 4, tile, 0)
        ds2[q, pos] = mine(q, pos, 0, 256, ho).astype(BF16)
        send(ds2.at[q, pos, top], dfl.at[q, r], ss.at[0], rs.at[0], right)
        send(ds2.at[q, pos, bot], dfr.at[q, r], ss.at[1], rs.at[1], left)
        dsr[q, pos, bot, :] = mine(q, pos, 128, 128, hr).astype(BF16)
        send(dsr.at[q, pos, bot], drl.at[q, r, bot], ss.at[2], rs.at[2], to_right(q))
        dsl[q, pos, top, :] = mine(q, pos, 0, 128, hl).astype(BF16)
        send(dsl.at[q, pos, top], drr.at[q, r, top], ss.at[3], rs.at[3], to_left(q))
        if q == 0:
            oacc[q, pos] = mine(q, pos, 0, 256, h).reshape(4, 64, 256)
            return

        @pl.when(home)
        def _():
            oacc[q, pos] = mine(q, pos, 0, 256, h).reshape(4, 64, 256)

        @pl.when(away)
        def _():
            dos[q, pos] = mine(q, pos, 0, 256, h).astype(BF16)
            last_copy(q, pos).start()

    def pass_right(q, pos):
        r = order[pos]
        ss, rs = d_s.at[q, pos], d_r.at[q, r]
        got(dfl.at[q, r], ss.at[0], rs.at[0])
        dsr[q, pos, top, :] = (mine(q, pos, 0, 128, hr) + dfl[q, r].astype(F32)).astype(BF16)
        send(dsr.at[q, pos, top], drl.at[q, r, top], ss.at[4], rs.at[4], to_right(q))

    def pass_left(q, pos):
        r = order[pos]
        ss, rs = d_s.at[q, pos], d_r.at[q, r]
        got(dfr.at[q, r], ss.at[1], rs.at[1])
        dsl[q, pos, bot, :] = (mine(q, pos, 128, 128, hl) + dfr[q, r].astype(F32)).astype(BF16)
        send(dsl.at[q, pos, bot], drr.at[q, r, bot], ss.at[5], rs.at[5], to_left(q))

    def write(q, pos):
        return pltpu.make_async_copy(oacc.at[q, pos], out.at[order[pos], :, q], o_s.at[q, pos])

    def finish(q, pos):
        r = order[pos]
        for i, ref in (
            (2, drl.at[q, r, bot]), (3, drr.at[q, r, top]), (4, drl.at[q, r, top]), (5, drr.at[q, r, bot])
        ):
            got(ref, d_s.at[q, pos, i], d_r.at[q, r, i])
        gathered = drl[q, r].astype(F32) + drr[q, r].astype(F32)

        @pl.when(home)
        def _():
            oacc[q, pos] = oacc[q, pos] + gathered.reshape(4, 64, 256)
            write(q, pos).start()

        @pl.when(away)
        def _():
            if q == 0:
                dos[q, pos] = (oacc[q, pos].reshape(256, 256) + gathered).astype(BF16)
                last_copy(q, pos).start()
            else:
                last_copy(q, pos).wait_recv()
                oacc[q, pos] = (dor[q, r].astype(F32) + gathered).reshape(4, 64, 256)
                write(q, pos).start()

    def land(q, pos):
        @pl.when(away)
        def _():
            last_copy(q, pos).wait_recv()
            oacc[q, pos] = dor[q, order[pos]].astype(F32).reshape(4, 64, 256)
            write(q, pos).start()

    ids_out()
    temporal_out(0)
    w_qkv.start()
    share_out()
    row = lax.broadcasted_iota(jnp.int32, (256, 256), 0)
    col = lax.broadcasted_iota(jnp.int32, (256, 256), 1)
    bias[...] = jnp.where((row % 16 == col % 16) & (row // 16 >= col // 16), 0.0, -1e30)
    temporal_pass(0)
    temporal_out(1)
    ids_spread()
    loads[0].wait()
    temporal_in(0)
    temporal_pass(1)
    proj_far(0)
    proj_near(0)
    proj_own(0)
    ready(0)
    ready(1)
    embed(0)
    proj_pass(0)
    temporal_in(1)
    proj_far(1)
    w_qkv.forward()
    own_send(0)
    for pos in range(3):
        w_qkv.take(pos)
    embed(1)
    ready(2)
    norm_one(0)
    proj_near(1)
    qkv(0, 0)
    qkv(0, 1)
    qkv(0, 2)
    w_qkv.take(3)
    qkv(0, 3)
    w_out.start()
    proj_own(1)
    attend(0, 0)
    attend(0, 1)
    w_out.forward()
    attend(0, 2)
    attend(0, 3)
    proj_pass(1)
    own_send(1)
    for pos in range(4):
        w_out.take(pos)
    out_proj(0)
    ready(3)
    ready(4)
    mlp(0, 0)
    norm_one(1)
    together(1)
    qkv(1, 0)
    ag_forward(*ag_two(0))
    qkv(1, 1)
    qkv(1, 2)
    qkv(1, 3)
    mlp(0, 1)
    mlp(0, 2)
    pass_right(0, 1)
    pass_left(0, 2)
    attend(1, 0)
    attend(1, 1)
    mlp(0, 3)
    attend(1, 2)
    attend(1, 3)
    pass_right(0, 3)
    pass_left(0, 0)
    pass_right(0, 0)
    pass_left(0, 3)
    pass_right(0, 2)
    pass_left(0, 1)
    out_proj(1)
    mlp(1, 0)
    for pos in (1, 2, 0, 3):
        finish(0, pos)
    ag_forward(*ag_two(1))
    mlp(1, 1)
    mlp(1, 2)
    pass_right(1, 1)
    pass_left(1, 2)
    for pos in range(4):
        land(0, pos)
    mlp(1, 3)
    pass_right(1, 3)
    pass_left(1, 0)
    pass_right(1, 0)
    pass_left(1, 3)
    pass_right(1, 2)
    pass_left(1, 1)
    for pos in (1, 2, 0, 3):
        finish(1, pos)

    for s in sends:
        s.wait_send()
    for q in range(2):
        for r in range(4):
            block = qs.at[q, r, pl.ds(0, 240)]
            rc(block, block, a_s.at[q, r], a_r.at[q, r], right).wait_send()
            block = att_s.at[q, r, pl.ds(0, 15)]
            rc(block, block, b_s.at[q, r], b_r.at[q, r], right).wait_send()

    @pl.when(home)
    def _():
        w_qkv.drain()
        w_out.drain()
        for i in range(5):
            share(i).wait_send()

    @pl.when(away)
    def _():
        for q in range(2):
            own_copy(q).wait_send()
            for pos in range(4):
                last_copy(q, pos).wait_send()

    for q in range(2):
        for pos in range(4):
            write(q, pos).wait()


def body(temporal, frame_ids, proj_weight, embed_table, qkv_weight, out_weight, gate_up, down_weight, norm_gains):
    vm, dma = pltpu.VMEM, pltpu.SemaphoreType.DMA
    any_spec = pl.BlockSpec(memory_space=pl.ANY)
    result = pl.pallas_call(
        kernel,
        name="depth_layer",
        out_shape=jax.ShapeDtypeStruct((4, 4, 2, 64, 256), F32),
        in_specs=[any_spec] * 8 + [pl.BlockSpec(memory_space=pltpu.VMEM)],
        out_specs=any_spec,
        scratch_shapes=[
            vm((2, 16, 64, 1024), BF16), vm((1024, 1024), BF16), vm((4, 3, 1024, 256), BF16), vm((4, 256, 1024), BF16),
            vm((2, 1024, 1024), BF16), vm((1024, 1024), BF16), vm((2, 256, 1024), BF16),
            vm((1, 1024), BF16), vm((4, 128), jnp.int32), vm((4, 128), jnp.int32),
            vm((2, 256, 128), jnp.int32), vm((256, 2048), BF16),
            vm((2, 256, 1024), BF16), vm((2, 256, 1024), BF16), vm((2, 256, 1024), BF16),
            vm((2, 128, 1024), BF16), vm((2, 128, 1024), BF16), vm((2, 256, 1024), BF16), vm((2, 256, 1024), BF16),
            vm((2, 256, 1024), F32),
            vm((2, 256, 1024), BF16), vm((2, 256, 1024), BF16), vm((2, 256, 1024), BF16), vm((2, 4, 256, 768), BF16), vm((2, 4, 16, 16, 768), BF16),
            vm((2, 4, 16, 16, 256), BF16), vm((2, 4, 256, 256), BF16), vm((256, 256), F32), vm((2, 1024), F32),
            vm((2, 4, 256, 1024), BF16), vm((2048, 1024), BF16),
            vm((2, 4, 256, 256), BF16), vm((2, 4, 256, 256), BF16), vm((2, 4, 256, 256), BF16),
            vm((2, 4, 128, 256), BF16), vm((2, 4, 128, 256), BF16),
            vm((2, 4, 256, 256), BF16), vm((2, 4, 256, 256), BF16),
            vm((2, 4, 256, 256), BF16), vm((2, 4, 256, 256), BF16), vm((2, 4, 4, 64, 256), F32),
            dma((10,)), dma((1,)), dma((1,)), dma((2, 15)), dma((2, 16)), dma((6,)), dma((6,)), dma((2, 6)), dma((2, 6)),
            dma((6,)), dma((6,)), dma((4,)), dma((4,)), dma((4,)), dma((4,)), dma((5,)), dma((5,)), dma((2, 4)), dma((2, 4)),
            dma((2,)), dma((2,)), dma((2, 6)), dma((2, 6)), dma((2, 4)), dma((2, 4)), dma((2, 4)), dma((2, 4)),
            dma((2, 4, 6)), dma((2, 4, 6)), dma((2, 4)), pltpu.SemaphoreType.REGULAR((2,)),
        ],
        compiler_params=pltpu.CompilerParams(
            collective_id=0, has_side_effects=True, vmem_limit_bytes=67043328
        ),
    )(
        temporal.reshape(2, 64, 1024), frame_ids.reshape(4, 4, 128), embed_table, proj_weight, qkv_weight, out_weight, gate_up, down_weight, norm_gains
    )
    return result.reshape(1, 2048, 256)


def solution(mesh):
    placed = (
        P(("frames", "codebook"), "hidden"),
        P("frames", "codebook"),
        P("codebook", "hidden", None),
        P("codebook", None, None),
        P("codebook", None, None, "hidden"),
        P("codebook", "hidden", None),
        P("codebook", None, None, "hidden"),
        P("codebook", "hidden", None),
        P("codebook", None, None),
    )
    return jax.shard_map(
        body,
        mesh=mesh,
        in_specs=placed,
        out_specs=P("codebook", "frames", "hidden"),
        check_vma=False,
    )
```

time: 211 us -> 176 us (0.83)
  Pallas kernels: 195 us -> 172 us
  local copies, waits for them, and re-layouts: 10.1 us -> 3.05 us
  starting transfers between devices: 4.49 us -> 0 us
    pallas_call x1, Pallas kernels: 195 us -> 172 us  [body(): pl.pallas_call(kernel, name='depth_layer', out_shape=jax.ShapeDtypeStruct...]
    gather x1 -> x0, local copies, waits for them, and re-layouts: 6.2 us -> none  [body(): emb = embed_table[0][previous].reshape(2, 256, 1024)]
    ppermute x1 -> x0, starting transfers between devices: 4.49 us -> none  [body(): earlier = lax.ppermute(own_ids, 'codebook', [(i, i + 1) for i in range(15)])]
  transfers between devices with their start and end apart: 1 -> 0, of which waited for: 1 -> 0; matrix products, arithmetic and copies ran while one was open for 0% -> 0% of each run, Pallas kernels for 0% -> 0%
where the time goes in v4:
time: 176 us; the launch traced here: 175 us
  Pallas kernels  172 us (98%)
  local copies, waits for them, and re-layouts  3.05 us (2%)
    pallas_call x1, Pallas kernels, body(): pl.pallas_call(kernel, name='depth_layer', out_shape=jax.ShapeDtypeStruct...  172 us

profile of v4, /device:TPU:1, one launch (start us, length us, event | category | flops | bytes accessed | tf_op | source)
XLA Modules:
  0.0 175.3 jit_solution(1655003989282845940)
XLA Ops:
  0.0 172.3 %depth_layer.1 = f32[4,4,2,64,256]{4,3,2,1,0:T(8,128)} custom-call(bf16[2,64,1024]{2,1,0:T(8,128)(2,1)} %bitcast.4, s32[4,4,128]{2,1,0:T(4,128)} %bitcast.5, bf16[1,2049,1024]{2,1,0:T(8,128)(2,1)} %table_in.1, bf16[1,1024,1024]{2,1,0:T(8,128)(2,1)} %wp_in.1, bf16[1,3,1024,256]{3,2,1,0:T(8,128)(2,1)} %wqkv_in.1, bf16[1,256,1024]{2,1,0:T(8,128)(2,1)} %wo_in.1, ...), custom_call_target="tpu_custom_call" | custom-call | tf_op jit(solution)/shard_map/depth_layer/pallas_call | solution.py:643
  172.3 3.0 %copy.11 = f32[1,2048,256]{2,1,0:T(8,128)} copy(f32[1,2048,256]{2,1,0:T(8,128)} %bitcast.3) | data formatting | bytes 4194304

commit v5 on v4

--- a/solution.py
+++ b/solution.py
@@ -94,11 +94,12 @@
     def share(i):
         return rc(common[i][0], common[i][1], g_s.at[i], g_r.at[i], partner)
 
-    def share_out():
+    def share_out(which):
         @pl.when(home)
         def _():
-            gain[...] = gains[0]
-            for i in range(5):
+            if 2 in which:
+                gain[...] = gains[0]
+            for i in which:
                 share(i).start()
 
     def ready(i):
@@ -207,30 +208,24 @@
     def proj_own(q):
         proj(q, h, 0, 256, into(x0.at[q], 0, 256))
 
-    def near_in(q):
-        got(prl.at[q, bot], p_s.at[q, 2], p_r.at[q, 2])
-        got(prr.at[q, top], p_s.at[q, 3], p_r.at[q, 3])
-
-    def own_send(q):
-        @pl.when(away)
-        def _():
-            near_in(q)
-            for half, near in ((top, prr), (bot, prl)):
-                own_s[q, half, :] = (x0[q, half, :] + near[q, half, :].astype(F32)).astype(BF16)
-            own_copy(q).start()
-
     def proj_pass(q):
         ss, rs = p_s.at[q], p_r.at[q]
         got(pfl.at[q], ss.at[0], rs.at[0])
         proj(q, hr, 0, 128, into(psr.at[q], 0, 128, pfl.at[q]))
-        send(psr.at[q, top], prl.at[q, top], ss.at[4], rs.at[4], owner(hr))
+        send(psr.at[q, top], prl.at[q, top], ss.at[4], rs.at[4], right)
         got(pfr.at[q], ss.at[1], rs.at[1])
         proj(q, hl, 128, 128, into(psl.at[q], 128, 128, pfr.at[q]))
-        send(psl.at[q, bot], prr.at[q, bot], ss.at[5], rs.at[5], owner(hl))
-
-    def norm_rows(q, dst, scale_by, base, extras, first_row=0, last_row=256):
+        send(psl.at[q, bot], prr.at[q, bot], ss.at[5], rs.at[5], left)
+
+    def row_chunks(step):
         def chunk(n, carry):
-            rows = pl.ds(pl.multiple_of(first_row + n * 32, 32), 32)
+            step(pl.ds(pl.multiple_of(n * 32, 32), 32))
+            return carry
+
+        lax.fori_loop(0, 8, chunk, 0)
+
+    def norm_rows(q, dst, scale_by, base, extras):
+        def step(rows):
             v = base[q, rows, :].astype(F32)
             for e in extras:
                 v = v + e[q, rows, :].astype(F32)
@@ -238,24 +233,31 @@
                 x0[q, rows, :] = v
             scale = lax.rsqrt(jnp.mean(v * v, axis=-1, keepdims=True) + 1e-05)
             dst[rows, :] = (v * scale * scale_by).astype(BF16)
-            return carry
-
-        lax.fori_loop(0, (last_row - first_row) // 32, chunk, 0)
+
+        row_chunks(step)
 
     def norm_one(q):
-        got(prl.at[q, top], p_s.at[q, 4], p_r.at[q, 4])
-        got(prr.at[q, bot], p_s.at[q, 5], p_r.at[q, 5])
+        for i, ref in ((2, prl.at[q, bot]), (3, prr.at[q, top]), (4, prl.at[q, top]), (5, prr.at[q, bot])):
+            got(ref, p_s.at[q, i], p_r.at[q, i])
 
         @pl.when(home)
         def _():
-            near_in(q)
             norm_rows(q, nq.at[q], gain[0:1, :], x0, (prl, prr, emb))
 
         @pl.when(away)
         def _():
+            def step(rows):
+                v = x0[q, rows, :] + prl[q, rows, :].astype(F32) + prr[q, rows, :].astype(F32)
+                own_s[q, rows, :] = v.astype(BF16)
+
+            row_chunks(step)
+            own_copy(q).start()
+
+    def x_in(q):
+        @pl.when(away)
+        def _():
             own_copy(q).wait_recv()
-            norm_rows(q, nq.at[q], gain[0:1, :], own_r, (prl, emb), 0, 128)
-            norm_rows(q, nq.at[q], gain[0:1, :], own_r, (prr, emb), 128, 256)
+            norm_rows(q, nq.at[q], gain[0:1, :], own_r, (emb,))
 
     def together(q):
         @pl.when(away)
@@ -316,7 +318,6 @@
                 loads[self.load].wait()
                 for i in (0, 2, 1, 3):
                     self.copy(i).start()
-                self.give(0).start()
 
         def forward(self):
             @pl.when(home)
@@ -326,14 +327,14 @@
                 self.arrive(2)
                 self.copy(5).start()
 
-        def take(self, pos):
+        def pull(self, pos):
             @pl.when(home)
             def _():
                 for i in ((), (1,), (3,), (4, 5))[pos]:
                     self.arrive(i)
-                if pos:
-                    self.give(pos).start()
-
+                self.give(pos).start()
+
+        def take(self, pos):
             @pl.when(away)
             def _():
                 self.give(pos).wait_recv()
@@ -519,7 +520,6 @@
     ids_out()
     temporal_out(0)
     w_qkv.start()
-    share_out()
     row = lax.broadcasted_iota(jnp.int32, (256, 256), 0)
     col = lax.broadcasted_iota(jnp.int32, (256, 256), 1)
     bias[...] = jnp.where((row % 16 == col % 16) & (row // 16 >= col // 16), 0.0, -1e30)
@@ -529,8 +529,10 @@
     loads[0].wait()
     temporal_in(0)
     temporal_pass(1)
+    share_out((0, 1, 2))
     proj_far(0)
     proj_near(0)
+    w_qkv.pull(0)
     proj_own(0)
     ready(0)
     ready(1)
@@ -539,34 +541,41 @@
     temporal_in(1)
     proj_far(1)
     w_qkv.forward()
-    own_send(0)
-    for pos in range(3):
-        w_qkv.take(pos)
+    w_qkv.pull(1)
+    w_qkv.pull(2)
     embed(1)
     ready(2)
     norm_one(0)
     proj_near(1)
+    x_in(0)
+    w_qkv.take(0)
     qkv(0, 0)
+    w_qkv.take(1)
     qkv(0, 1)
+    w_qkv.take(2)
     qkv(0, 2)
+    w_qkv.pull(3)
     w_qkv.take(3)
     qkv(0, 3)
     w_out.start()
+    share_out((3, 4))
     proj_own(1)
+    proj_pass(1)
     attend(0, 0)
     attend(0, 1)
     w_out.forward()
     attend(0, 2)
     attend(0, 3)
-    proj_pass(1)
-    own_send(1)
+    norm_one(1)
+    for pos in range(4):
+        w_out.pull(pos)
     for pos in range(4):
         w_out.take(pos)
     out_proj(0)
     ready(3)
     ready(4)
     mlp(0, 0)
-    norm_one(1)
+    x_in(1)
     together(1)
     qkv(1, 0)
     ag_forward(*ag_two(0))

time: 176 us -> 171 us (0.972)
  Pallas kernels: 172 us -> 167 us
    pallas_call x1, Pallas kernels: 172 us -> 167 us  [body(): pl.pallas_call(kernel, name='depth_layer', out_shape=jax.ShapeDtypeStruct...]
where the time goes in v5:
time: 171 us; the launch traced here: 170 us
  Pallas kernels  167 us (98%)
  local copies, waits for them, and re-layouts  3.05 us (2%)
    pallas_call x1, Pallas kernels, body(): pl.pallas_call(kernel, name='depth_layer', out_shape=jax.ShapeDtypeStruct...  167 us

profile of v5, /device:TPU:1, one launch (start us, length us, event | category | flops | bytes accessed | tf_op | source)
XLA Modules:
  0.0 170.4 jit_solution(7862906933144573981)
XLA Ops:
  0.0 167.4 %depth_layer.1 = f32[4,4,2,64,256]{4,3,2,1,0:T(8,128)} custom-call(bf16[2,64,1024]{2,1,0:T(8,128)(2,1)} %bitcast.4, s32[4,4,128]{2,1,0:T(4,128)} %bitcast.5, bf16[1,2049,1024]{2,1,0:T(8,128)(2,1)} %table_in.1, bf16[1,1024,1024]{2,1,0:T(8,128)(2,1)} %wp_in.1, bf16[1,3,1024,256]{3,2,1,0:T(8,128)(2,1)} %wqkv_in.1, bf16[1,256,1024]{2,1,0:T(8,128)(2,1)} %wo_in.1, ...), custom_call_target="tpu_custom_call" | custom-call | tf_op jit(solution)/shard_map/depth_layer/pallas_call | solution.py:652
  167.4 3.0 %copy.11 = f32[1,2048,256]{2,1,0:T(8,128)} copy(f32[1,2048,256]{2,1,0:T(8,128)} %bitcast.3) | data formatting | bytes 4194304
